TPU v7x, 32 devices: a whole 2x2x4 slice. The times are simulated.
32 devices in a mesh: dp: 16 (over z, y, core), mp: 2 (over x).
Axes of the slice: x: 2, y: 2, z: 4, core: 2. Of those that a mesh axis runs over, the one named last changes fastest.
Arguments:
- activations: bfloat16 [8192, 28672], P('dp', 'mp'), may hold values from -200 to 200
- weight: bfloat16 [8192, 28672], P(None, ('mp', 'dp')), may hold values from -25 to 25
- thresholds: float32 [8192], P('dp'), may hold values from 0.5 to 1.5
Outputs:
- pruned: bfloat16 [8192, 28672], P('dp', 'mp')
All inputs are finite; a program needn't handle non-finite values.
Results may differ from a plain program's by a relative error of at most 0.0004.
Values may be sent and summed in bfloat16 or wider, within the bound.
No kernel may reach another device: no remote copies, remote signals or barrier semaphores. Data moves between devices by JAX's collectives and lax.ppermute only.
A program may use at most 128 MiB of HBM per device.

v0:
```python
import jax
import jax.numpy as jnp
from jax import lax
from jax.sharding import PartitionSpec as P

IN = 28672


gate_slope = 2.0
small_eps = 1e-06


def soft_prune(block, col_norm, row_total, limit):
    wide = block.astype(jnp.float32)
    scores = jnp.abs(wide) * col_norm[None, :]
    row_mean = row_total[:, None] / IN + small_eps
    kept_share = jnp.clip((scores / row_mean - limit[:, None]) * gate_slope + 0.5, 0.0, 1.0)
    return (wide * kept_share).astype(jnp.bfloat16)


def per_device(activations, weight, thresholds):
    partial_value = jnp.sum(jnp.square(activations.astype(jnp.float32)), axis=0)
    relaid = lax.all_to_all(weight, "dp", split_axis=0, concat_axis=1, tiled=True)
    squares = lax.psum(partial_value, "dp")
    col_norm = jnp.sqrt(squares)
    row_part = jnp.sum(jnp.abs(relaid.astype(jnp.float32)) * col_norm[None, :], axis=1)
    row_total = lax.psum(row_part, "mp")
    return soft_prune(relaid, col_norm, row_total, thresholds)


def solution(mesh):
    placed = (P("dp", "mp"), P(None, ("mp", "dp")), P("dp"))
    return jax.shard_map(
        per_device, mesh=mesh, in_specs=placed, out_specs=P("dp", "mp"), check_vma=False
    )
```

profile of v0, /device:TPU:0, one launch (start us, length us, event | category | flops | bytes accessed | tf_op | source)
XLA Modules:
  0.0 432.1 jit_solution(9146727415281544940)
XLA Ops:
  0.0 7.5 %all-to-all-start = ((bf16[16,512,896]{2,1,0:T(8,128)(2,1)}), bf16[16,512,896]{2,1,0:T(8,128)(2,1)}, u32[]{:S(2)}, u32[]{:S(2)}) async-start(bf16[16,512,896]{2,1,0:T(8,128)(2,1)} %bitcast.22), calls=%async_computation | async-start | bytes 29360128 | tf_op jit(solution)/shard_map/all_to_all | solution.py:23
  7.5 8.5 %multiply_reduce_fusion = f32[14336]{0:T(1024)S(1)} fusion(bf16[512,14336]{1,0:T(8,128)(2,1)} %param.3), kind=kLoop, calls=%fused_computation.12 | loop fusion | flops 22005760 | bytes 14737408 | tf_op jit(solution)/shard_map/reduce_sum | solution.py:22
  16.0 347.7 %psum.14 = f32[14336]{0:T(1024)S(1)} all-reduce(f32[14336]{0:T(1024)S(1)} %multiply_reduce_fusion), channel_id=1, replica_groups=mesh['dp'=16,'mp'=2] {'dp'}, use_global_device_ids=true, to_apply=%region_1.0 | all-reduce | flops 14336 | bytes 114688 | tf_op jit(solution)/shard_map/psum | solution.py:24
  363.7 0.0 all-to-all-done
  363.7 20.7 %copy.5 = bf16[16,512,896]{1,2,0:T(8,128)(2,1)} copy(bf16[16,512,896]{2,1,0:T(8,128)(2,1)} %all-to-all-done) | data formatting | bytes 29360128 | tf_op jit(solution)/shard_map/all_to_all | solution.py:23
  384.4 0.0 copy-start
  384.4 6.9 %fusion.1 = f32[512]{0:T(512)S(1)} fusion(bf16[16,512,896]{1,2,0:T(8,128)(2,1)} %copy.5, f32[16,896]{1,0:T(8,128)S(1)} %mul.31), kind=kLoop, calls=%fused_computation.4 | loop fusion | flops 29359616 | bytes 14739456 | tf_op jit(solution)/shard_map/reduce_sum | solution.py:26
  391.3 4.9 %psum.15 = f32[512]{0:T(512)S(1)} all-reduce(f32[512]{0:T(512)S(1)} %fusion.1), channel_id=1, replica_groups=mesh['dp'=16,'mp'=2] {'mp'}, use_global_device_ids=true, to_apply=%region_3.0 | all-reduce | flops 512 | bytes 4096 | tf_op jit(solution)/shard_map/psum | solution.py:27
  396.2 0.0 copy-done
  396.2 16.0 %fusion.8 = bf16[512,14336]{0,1:T(8,128)(2,1)} fusion(bf16[16,512,896]{1,2,0:T(8,128)(2,1)} %copy.5, f32[512]{0:T(512)S(1)} %copy-done, f32[512]{0:T(512)S(1)} %multiply_add_fusion, f32[14336]{0:T(1024)S(1)} %sqrt.3), kind=kLoop, calls=%fused_computation.11 | loop fusion | flops 73400320 | bytes 29421568 | tf_op jit(solution)/shard_map/convert_element_type | solution.py:18
  412.2 19.9 %copy.6 = bf16[512,14336]{1,0:T(8,128)(2,1)} copy(bf16[512,14336]{0,1:T(8,128)(2,1)} %fusion.8) | data formatting | bytes 29360128 | tf_op jit(solution)/shard_map/convert_element_type | solution.py:18
  (3 shorter events, 0.0 us)
Async XLA Ops:
  0.0 363.7 %all-to-all-start = ((bf16[16,512,896]{2,1,0:T(8,128)(2,1)}), bf16[16,512,896]{2,1,0:T(8,128)(2,1)}, u32[]{:S(2)}, u32[]{:S(2)}) async-start(bf16[16,512,896]{2,1,0:T(8,128)(2,1)} %bitcast.22), calls=%async_computation | async-start | bytes 29360128 | tf_op jit(solution)/shard_map/all_to_all | solution.py:23
  384.4 11.9 %copy-start = (f32[512]{0:T(512)S(1)}, f32[512]{0:T(512)}, u32[]{:S(2)}) copy-start(f32[512]{0:T(512)} %param.5) | copy-start | bytes 6148
where the time goes:
time: 434 us; the launch traced here: 432 us
  blocking collectives  353 us (81%)
  local copies, waits for them, and re-layouts  40.6 us (9%)
  other arithmetic  31.4 us (7%)
  starting transfers between devices  7.46 us (2%)
    psum x1, blocking collectives, per_device(): squares = lax.psum(partial_value, 'dp')  348 us
    all_to_all x1, local copies, waits for them, and re-layouts, per_device(): lax.all_to_all(weight, 'dp', split_axis=0, concat_axis=1, tiled=True)  20.7 us
    convert_element_type x1, local copies, waits for them, and re-layouts, soft_prune(): return (wide * kept_share).astype(jnp.bfloat16)  19.9 us
    convert_element_type x1, other arithmetic, soft_prune(): return (wide * kept_share).astype(jnp.bfloat16)  16 us
  transfers between devices with their start and end apart: 1, of which 0 were waited for; matrix products, arithmetic and copies ran while one was open for 2% of the time, Pallas kernels for 0%

commit v1 on v0

v1 whole, which is shorter than its diff:
```python
import functools

import jax
import jax.numpy as jnp
import numpy as np
from jax import lax
from jax.experimental import pallas as pl
from jax.experimental.pallas import tpu as pltpu
from jax.sharding import PartitionSpec as P


gate_slope = 2.0
small_eps = 1e-06


def exchange_plan(n):
    if n != 16:
        if n & (n - 1) == 0:
            return [[i ^ s for i in range(n)] for s in list(range(n // 2, n)) + list(range(n // 2))]
        return [[(i + s) % n for i in range(n)] for s in range(n)]
    plan = []
    for o, q in zip((0, 1, 2, 3), (1, 2, 3, 0)):
        plan.append([(12 - 4 * (i // 4)) + (i % 4 ^ o) if i // 4 in (1, 2) else i ^ q for i in range(n)])
    for hop in ((1, 3, 0, 2), (2, 0, 3, 1)):
        for o in (0, 1, 2, 3):
            plan.append([4 * hop[i // 4] + (i % 4 ^ o) for i in range(n)])
    for o, q in zip((0, 1, 2, 3), (1, 2, 3, 0)):
        plan.append([(12 - 4 * (i // 4)) + (i % 4 ^ o) if i // 4 in (0, 3) else i ^ q for i in range(n)])
    return plan


def take_block(table, weight, step, rows):
    cols = weight.shape[1]
    tile = rows // 4 if rows % 64 == 0 else rows

    def body(_, src, dst):
        dst[...] = src[...]

    return pl.pallas_call(
        body,
        grid_spec=pltpu.PrefetchScalarGridSpec(
            num_scalar_prefetch=1,
            grid=(rows // tile,),
            in_specs=[pl.BlockSpec((tile, cols), lambda r, t: (t[step] * (rows // tile) + r, 0))],
            out_specs=pl.BlockSpec((tile, cols), lambda r, t: (r, 0)),
        ),
        out_shape=jax.ShapeDtypeStruct((rows, cols), weight.dtype),
        cost_estimate=pl.CostEstimate(flops=0, bytes_accessed=4 * rows * cols, transcendentals=0),
    )(table, weight)


def prune_block(table, block, norm, slope, shift, step, n, out):
    rows, cols = block.shape
    tile = rows // 4 if rows % 64 == 0 else rows

    def body(_, block_ref, norm_ref, slope_ref, shift_ref, *rest):
        wide = block_ref[...].astype(jnp.float32)
        scores = jnp.abs(wide) * norm_ref[...]
        share = jnp.clip(scores * slope_ref[...] + shift_ref[...], 0.0, 1.0)
        rest[-1][...] = (wide * share).astype(jnp.bfloat16)

    in_specs = [
        pl.BlockSpec((tile, cols), lambda r, t: (r, 0)),
        pl.BlockSpec((1, cols), lambda r, t: (0, 0)),
        pl.BlockSpec((tile, 1), lambda r, t: (r, 0)),
        pl.BlockSpec((tile, 1), lambda r, t: (r, 0)),
    ]
    operands = [table, block, norm, slope, shift]
    aliases = {}
    if out is not None:
        in_specs.append(pl.BlockSpec(memory_space=pl.ANY))
        operands.append(out)
        aliases = {5: 0}
    return pl.pallas_call(
        body,
        grid_spec=pltpu.PrefetchScalarGridSpec(
            num_scalar_prefetch=1,
            grid=(rows // tile,),
            in_specs=in_specs,
            out_specs=pl.BlockSpec((tile, cols), lambda r, t: (r, t[step])),
        ),
        out_shape=jax.ShapeDtypeStruct((rows, n * cols), jnp.bfloat16),
        input_output_aliases=aliases,
        cost_estimate=pl.CostEstimate(flops=6 * rows * cols, bytes_accessed=4 * rows * cols, transcendentals=0),
    )(*operands)


def per_device(n, n_mp, activations, weight, thresholds):
    plan = exchange_plan(n)
    targets = np.array(plan, np.int32).T
    sources = np.stack([np.argsort(p) for p in plan]).astype(np.int32).T
    me = lax.axis_index("dp")
    to = lax.dynamic_index_in_dim(jnp.asarray(targets), me, 0, keepdims=False)
    come = lax.dynamic_index_in_dim(jnp.asarray(sources), me, 0, keepdims=False)
    cols = weight.shape[1]
    rows = weight.shape[0] // n
    total_cols = cols * n * n_mp

    def send(x, step):
        return lax.ppermute(x, "dp", [(i, plan[step][i]) for i in range(n)])

    blocks = []
    for k in range(n):
        blocks.append(take_block(to, weight, k, rows))
    arrived = [send(blocks[k], k) for k in range(n)]

    partial_value = jnp.sum(jnp.square(activations.astype(jnp.float32)), axis=0)
    parts = jnp.take(partial_value.reshape(n, cols), to, axis=0)
    got = [send(parts[k], k) for k in range(n)]
    col_norm = jnp.sqrt(functools.reduce(jnp.add, got))
    row_part = jnp.sum(jnp.abs(weight.astype(jnp.float32)) * col_norm[None, :], axis=1).reshape(n, rows)
    notes = jnp.concatenate([jnp.take(row_part, to, axis=0), jnp.broadcast_to(col_norm, (n, cols))], axis=1)
    noted = [send(notes[k], k) for k in range(n)]
    row_total = lax.psum(functools.reduce(jnp.add, [v[:rows] for v in noted]), "mp")
    row_mean = row_total / total_cols + small_eps
    slope = (gate_slope / row_mean)[:, None]
    shift = (0.5 - gate_slope * thresholds)[:, None]

    if cols % 128 == 0:
        out = None
        late = list(range(n // 2 - 2, n // 2))
        for k in [v for v in range(n) if v not in late] + late:
            out = prune_block(come, arrived[k], noted[k][rows:][None, :], slope, shift, k, n, out)
        return out
    out = jnp.zeros((rows, n * cols), jnp.bfloat16)
    for k in range(n):
        wide = arrived[k].astype(jnp.float32)
        share = jnp.clip(jnp.abs(wide) * noted[k][None, rows:] * slope + shift, 0.0, 1.0)
        out = lax.dynamic_update_slice(out, (wide * share).astype(jnp.bfloat16), (0, come[k] * cols))
    return out


def solution(mesh):
    placed = (P("dp", "mp"), P(None, ("mp", "dp")), P("dp"))
    return jax.shard_map(
        functools.partial(per_device, mesh.shape["dp"], mesh.shape["mp"]),
        mesh=mesh,
        in_specs=placed,
        out_specs=P("dp", "mp"),
        check_vma=False,
    )
```

time: 434 us -> 396 us (0.912)
  blocking collectives: 353 us -> 5.11 us
  Pallas kernels: 0 us -> 134 us
  waiting for transfers between devices: 0.01 us -> 126 us
  starting transfers between devices: 7.46 us -> 89.1 us
  local copies, waits for them, and re-layouts: 40.6 us -> 17.2 us
  other arithmetic: 31.4 us -> 21.2 us
    psum x2 -> x1, blocking collectives: 353 us -> 5.11 us  [per_device(): lax.psum(functools.reduce(jnp.add, [v[:rows] for v in noted]), 'mp')]
    pallas_call x0 -> x32, Pallas kernels: none -> 134 us  [the longest x16 69.9 us: prune_block(): pl.pallas_call(body, grid_spec=pltpu.PrefetchScalarGridSpec(num_scalar_pr...]
    ppermute x0 -> x48, waiting for transfers between devices: none -> 126 us  [send(): return lax.ppermute(x, 'dp', [(i, plan[step][i]) for i in range(n)])]
    ppermute x0 -> x48, starting transfers between devices: none -> 89.1 us  [send(): return lax.ppermute(x, 'dp', [(i, plan[step][i]) for i in range(n)])]
    all_to_all x1 -> x0, local copies, waits for them, and re-layouts: 20.7 us -> none  [per_device(): lax.all_to_all(weight, 'dp', split_axis=0, concat_axis=1, tiled=True)]
    convert_element_type x1 -> x0, local copies, waits for them, and re-layouts: 19.9 us -> none  [soft_prune(): return (wide * kept_share).astype(jnp.bfloat16)]
    convert_element_type x1 -> x0, other arithmetic: 16 us -> none  [soft_prune(): return (wide * kept_share).astype(jnp.bfloat16)]
    broadcast_in_dim x0 -> x18, local copies, waits for them, and re-layouts: none -> 11.2 us  [the longest x16 9.5 us: per_device(): noted[k][rows:][None, :]]
  transfers between devices with their start and end apart: 1 -> 48, of which waited for: 0 -> 7; matrix products, arithmetic and copies ran while one was open for 2% -> 7% of each run, Pallas kernels for 0% -> 33%
where the time goes in v1:
time: 396 us; the launch traced here: 393 us
  Pallas kernels  134 us (34%)
  waiting for transfers between devices  126 us (32%)
  starting transfers between devices  89.1 us (22%)
  other arithmetic  21.2 us (5%)
  local copies, waits for them, and re-layouts  17.2 us (4%)
  blocking collectives  5.11 us (1%)
    ppermute x48, waiting for transfers between devices, send(): return lax.ppermute(x, 'dp', [(i, plan[step][i]) for i in range(n)])  126 us
    ppermute x48, starting transfers between devices, send(): return lax.ppermute(x, 'dp', [(i, plan[step][i]) for i in range(n)])  89.1 us
    pallas_call x16, Pallas kernels, prune_block(): pl.pallas_call(body, grid_spec=pltpu.PrefetchScalarGridSpec(num_scalar_pr...  69.9 us
    pallas_call x16, Pallas kernels, take_block(): pl.pallas_call(body, grid_spec=pltpu.PrefetchScalarGridSpec(num_scalar_pr...  64 us
    reduce_sum x1, other arithmetic, per_device(): jnp.sum(jnp.abs(weight.astype(jnp.float32)) * col_norm[None, :], axis=1)  11.1 us
    broadcast_in_dim x16, local copies, waits for them, and re-layouts, per_device(): noted[k][rows:][None, :]  9.5 us
    reduce_sum x1, other arithmetic, per_device(): partial_value = jnp.sum(jnp.square(activations.astype(jnp.float32)), axis=0)  8.52 us
  transfers between devices with their start and end apart: 48, of which 7 were waited for; matrix products, arithmetic and copies ran while one was open for 7% of the time, Pallas kernels for 33%

profile of v1, /device:TPU:0, one launch (start us, length us, event | category | flops | bytes accessed | tf_op | source)
XLA Modules:
  0.0 392.7 jit_solution(16141380603016369639)
XLA Ops:
  1.4 8.5 %multiply_reduce_fusion.1 = f32[14336]{0:T(1024)S(1)} fusion(bf16[512,14336]{1,0:T(8,128)(2,1)} %param.5), kind=kLoop, calls=%fused_computation.3 | loop fusion | flops 22005760 | bytes 14737408 | tf_op jit(solution)/shard_map/reduce_sum | solution.py:107
  24.0 4.6 %collective-permute-start.16 = (f32[896]{0:T(1024)S(1)}, f32[896]{0:T(1024)S(1)}, u32[]{:S(2)}, u32[]{:S(2)}) collective-permute-start(f32[896]{0:T(1024)S(1)} %get-tuple-element.22), channel_id=1, source_target_pairs={{0,30},{2,28},{4,26},{6,24},{8,8},{10,10},{12,12},{14,14},{16,16},... | collective-permute-start | bytes 10760 | tf_op jit(solution)/shard_map/ppermute | solution.py:100
  43.9 11.1 %multiply_reduce_fusion = f32[8192]{0:T(1024)S(1)} fusion(bf16[8192,896]{1,0:T(8,128)(2,1)} %src.31, f32[896]{0:T(1024)S(1)} %add_sqrt_fusion), kind=kLoop, calls=%fused_computation.2 | loop fusion | flops 29351936 | bytes 14716416 | tf_op jit(solution)/shard_map/reduce_sum | solution.py:111
  58.6 8.0 %collective-permute-done.17 = f32[1408]{0:T(1024)S(1)} collective-permute-done((f32[1408]{0:T(1024)S(1)}, f32[1408]{0:T(1024)S(1)}, u32[]{:S(2)}, u32[]{:S(2)}) %collective-permute-start.17) | collective-permute-done | bytes 5664 | tf_op jit(solution)/shard_map/ppermute | solution.py:100
  99.6 8.3 %collective-permute-start.44 = (bf16[512,896]{1,0:T(8,128)(2,1)}, bf16[512,896]{1,0:T(8,128)(2,1)}, u32[]{:S(2)}, u32[]{:S(2)}) collective-permute-start(bf16[512,896]{1,0:T(8,128)(2,1)} %shard_map.67), channel_id=1, source_target_pairs={{0,0},{2,2},{4,4},{6,6},{8,22},{10,20},{12,18},{14,16},{16,14},{18... | collective-permute-start | bytes 2752520 | tf_op jit(solution)/shard_map/ppermute | solution.py:100
  135.5 13.1 %collective-permute-start.39 = (bf16[512,896]{1,0:T(8,128)(2,1)}, bf16[512,896]{1,0:T(8,128)(2,1)S(1)}, u32[]{:S(2)}, u32[]{:S(2)}) collective-permute-start(bf16[512,896]{1,0:T(8,128)(2,1)} %shard_map.62), channel_id=1, source_target_pairs={{0,20},{2,22},{4,16},{6,18},{8,4},{10,6},{12,0},{14,2},{16,28},{18... | collective-permute-start | bytes 2752520 | tf_op jit(solution)/shard_map/ppermute | solution.py:100
  152.6 74.2 %collective-permute-done.43.block_ref = bf16[512,896]{1,0:T(8,128)(2,1)} collective-permute-done((bf16[512,896]{1,0:T(8,128)(2,1)}, bf16[512,896]{1,0:T(8,128)(2,1)}, u32[]{:S(2)}, u32[]{:S(2)}) %collective-permute-start.43) | collective-permute-done | bytes 917536 | tf_op jit(solution)/shard_map/ppermute | solution.py:100
  230.8 33.0 %collective-permute-done.42.block_ref = bf16[512,896]{1,0:T(8,128)(2,1)} collective-permute-done((bf16[512,896]{1,0:T(8,128)(2,1)}, bf16[512,896]{1,0:T(8,128)(2,1)}, u32[]{:S(2)}, u32[]{:S(2)}) %collective-permute-start.42) | collective-permute-done | bytes 917536 | tf_op jit(solution)/shard_map/ppermute | solution.py:100
  299.9 5.1 %psum.7 = f32[512]{0:T(512)S(1)} all-reduce(f32[512]{0:T(512)S(1)} %slice_add_fusion), channel_id=1, replica_groups=mesh['dp'=16,'mp'=2] {'mp'}, use_global_device_ids=true, to_apply=%region_2.3 | all-reduce | flops 512 | bytes 4096 | tf_op jit(solution)/shard_map/psum | solution.py:114
  315.5 4.4 %shard_map.71.rest_0_ = bf16[512,14336]{1,0:T(8,128)(2,1)} custom-call(s32[16]{0:T(128)} %dynamic-slice_bitcast_fusion._, bf16[512,896]{1,0:T(8,128)(2,1)} %copy-done, f32[1,896]{1,0:T(1,128)} %broadcast_in_dim.100.norm_ref, f32[512,1]{1,0:T(8,128)} %copy.51.slope_ref, f32[512,1]{1,0:T(8,128)} %copy.52.shift_ref), custom_call_target="tpu_custom_call" | custom-call | flops 2752512 | bytes 1835008 | tf_op jit(solution)/shard_map/pallas_call | solution.py:74
  319.8 4.4 %shard_map.72.rest_0_ = bf16[512,14336]{1,0:T(8,128)(2,1)} custom-call(s32[16]{0:T(128)} %dynamic-slice_bitcast_fusion._, bf16[512,896]{1,0:T(8,128)(2,1)} %copy-done.1, f32[1,896]{1,0:T(1,128)} %broadcast_in_dim.99.norm_ref, f32[512,1]{1,0:T(8,128)} %copy.51.slope_ref, f32[512,1]{1,0:T(8,128)} %copy.52.shift_ref, ...), custom_call_target="tpu_custom_call", output_to_operand_aliasing={{}: (5, {})} | custom-call | flops 2752512 | bytes 1835008 | tf_op jit(solution)/shard_map/pallas_call | solution.py:74
  324.2 4.4 %shard_map.73.rest_0_ = bf16[512,14336]{1,0:T(8,128)(2,1)} custom-call(s32[16]{0:T(128)} %dynamic-slice_bitcast_fusion._, bf16[512,896]{1,0:T(8,128)(2,1)} %copy-done.2, f32[1,896]{1,0:T(1,128)} %broadcast_in_dim.98.norm_ref, f32[512,1]{1,0:T(8,128)} %copy.51.slope_ref, f32[512,1]{1,0:T(8,128)} %copy.52.shift_ref, ...), custom_call_target="tpu_custom_call", output_to_operand_aliasing={{}: (5, {})} | custom-call | flops 2752512 | bytes 1835008 | tf_op jit(solution)/shard_map/pallas_call | solution.py:74
  328.6 4.4 %shard_map.74.rest_0_ = bf16[512,14336]{1,0:T(8,128)(2,1)} custom-call(s32[16]{0:T(128)} %dynamic-slice_bitcast_fusion._, bf16[512,896]{1,0:T(8,128)(2,1)} %collective-permute-done.44.block_ref, f32[1,896]{1,0:T(1,128)} %broadcast_in_dim.97.norm_ref, f32[512,1]{1,0:T(8,128)} %copy.51.slope_ref, ...), custom_call_target="tpu_custom_call", output_to_operand_aliasing={{}: (5, {})} | custom-call | flops 2752512 | bytes 1835008 | tf_op jit(solution)/shard_map/pallas_call | solution.py:74
  333.0 4.4 %shard_map.75.rest_0_ = bf16[512,14336]{1,0:T(8,128)(2,1)} custom-call(s32[16]{0:T(128)} %dynamic-slice_bitcast_fusion._, bf16[512,896]{1,0:T(8,128)(2,1)} %collective-permute-done.43.block_ref, f32[1,896]{1,0:T(1,128)} %broadcast_in_dim.96.norm_ref, f32[512,1]{1,0:T(8,128)} %copy.51.slope_ref, ...), custom_call_target="tpu_custom_call", output_to_operand_aliasing={{}: (5, {})} | custom-call | flops 2752512 | bytes 1835008 | tf_op jit(solution)/shard_map/pallas_call | solution.py:74
  337.3 4.4 %shard_map.76.rest_0_ = bf16[512,14336]{1,0:T(8,128)(2,1)} custom-call(s32[16]{0:T(128)} %dynamic-slice_bitcast_fusion._, bf16[512,896]{1,0:T(8,128)(2,1)} %collective-permute-done.42.block_ref, f32[1,896]{1,0:T(1,128)} %broadcast_in_dim.95.norm_ref, f32[512,1]{1,0:T(8,128)} %copy.51.slope_ref, ...), custom_call_target="tpu_custom_call", output_to_operand_aliasing={{}: (5, {})} | custom-call | flops 2752512 | bytes 1835008 | tf_op jit(solution)/shard_map/pallas_call | solution.py:74
  350.4 4.4 %shard_map.79.rest_0_ = bf16[512,14336]{1,0:T(8,128)(2,1)} custom-call(s32[16]{0:T(128)} %dynamic-slice_bitcast_fusion._, bf16[512,896]{1,0:T(8,128)(2,1)} %copy-done.4, f32[1,896]{1,0:T(1,128)} %broadcast_in_dim.92.norm_ref, f32[512,1]{1,0:T(8,128)} %copy.51.slope_ref, f32[512,1]{1,0:T(8,128)} %copy.52.shift_ref, ...), custom_call_target="tpu_custom_call", output_to_operand_aliasing={{}: (5, {})} | custom-call | flops 2752512 | bytes 1835008 | tf_op jit(solution)/shard_map/pallas_call | solution.py:74
  354.8 4.4 %shard_map.80.rest_0_ = bf16[512,14336]{1,0:T(8,128)(2,1)} custom-call(s32[16]{0:T(128)} %dynamic-slice_bitcast_fusion._, bf16[512,896]{1,0:T(8,128)(2,1)} %copy-done.5, f32[1,896]{1,0:T(1,128)} %broadcast_in_dim.91.norm_ref, f32[512,1]{1,0:T(8,128)} %copy.51.slope_ref, f32[512,1]{1,0:T(8,128)} %copy.52.shift_ref, ...), custom_call_target="tpu_custom_call", output_to_operand_aliasing={{}: (5, {})} | custom-call | flops 2752512 | bytes 1835008 | tf_op jit(solution)/shard_map/pallas_call | solution.py:74
  359.2 4.4 %shard_map.81.rest_0_ = bf16[512,14336]{1,0:T(8,128)(2,1)} custom-call(s32[16]{0:T(128)} %dynamic-slice_bitcast_fusion._, bf16[512,896]{1,0:T(8,128)(2,1)} %collective-permute-done.37.block_ref, f32[1,896]{1,0:T(1,128)} %broadcast_in_dim.90.norm_ref, f32[512,1]{1,0:T(8,128)} %copy.51.slope_ref, ...), custom_call_target="tpu_custom_call", output_to_operand_aliasing={{}: (5, {})} | custom-call | flops 2752512 | bytes 1835008 | tf_op jit(solution)/shard_map/pallas_call | solution.py:74
  363.6 4.4 %shard_map.82.rest_0_ = bf16[512,14336]{1,0:T(8,128)(2,1)} custom-call(s32[16]{0:T(128)} %dynamic-slice_bitcast_fusion._, bf16[512,896]{1,0:T(8,128)(2,1)} %collective-permute-done.36.block_ref, f32[1,896]{1,0:T(1,128)} %broadcast_in_dim.89.norm_ref, f32[512,1]{1,0:T(8,128)} %copy.51.slope_ref, ...), custom_call_target="tpu_custom_call", output_to_operand_aliasing={{}: (5, {})} | custom-call | flops 2752512 | bytes 1835008 | tf_op jit(solution)/shard_map/pallas_call | solution.py:74
  367.9 4.4 %shard_map.83.rest_0_ = bf16[512,14336]{1,0:T(8,128)(2,1)} custom-call(s32[16]{0:T(128)} %dynamic-slice_bitcast_fusion._, bf16[512,896]{1,0:T(8,128)(2,1)} %collective-permute-done.35.block_ref, f32[1,896]{1,0:T(1,128)} %broadcast_in_dim.88.norm_ref, f32[512,1]{1,0:T(8,128)} %copy.51.slope_ref, ...), custom_call_target="tpu_custom_call", output_to_operand_aliasing={{}: (5, {})} | custom-call | flops 2752512 | bytes 1835008 | tf_op jit(solution)/shard_map/pallas_call | solution.py:74
  372.3 4.4 %shard_map.84.rest_0_ = bf16[512,14336]{1,0:T(8,128)(2,1)} custom-call(s32[16]{0:T(128)} %dynamic-slice_bitcast_fusion._, bf16[512,896]{1,0:T(8,128)(2,1)} %collective-permute-done.34.block_ref, f32[1,896]{1,0:T(1,128)} %broadcast_in_dim.87.norm_ref, f32[512,1]{1,0:T(8,128)} %copy.51.slope_ref, ...), custom_call_target="tpu_custom_call", output_to_operand_aliasing={{}: (5, {})} | custom-call | flops 2752512 | bytes 1835008 | tf_op jit(solution)/shard_map/pallas_call | solution.py:74
  377.6 4.4 %shard_map.85.rest_0_ = bf16[512,14336]{1,0:T(8,128)(2,1)} custom-call(s32[16]{0:T(128)} %dynamic-slice_bitcast_fusion._, bf16[512,896]{1,0:T(8,128)(2,1)} %copy-done.6, f32[1,896]{1,0:T(1,128)} %broadcast_in_dim.86.norm_ref, f32[512,1]{1,0:T(8,128)} %copy.51.slope_ref, f32[512,1]{1,0:T(8,128)} %copy.52.shift_ref, ...), custom_call_target="tpu_custom_call", output_to_operand_aliasing={{}: (5, {})} | custom-call | flops 2752512 | bytes 1835008 | tf_op jit(solution)/shard_map/pallas_call | solution.py:74
  382.0 5.4 %collective-permute-done.block_ref = bf16[512,896]{1,0:T(8,128)(2,1)S(1)} collective-permute-done((bf16[512,896]{1,0:T(8,128)(2,1)}, bf16[512,896]{1,0:T(8,128)(2,1)S(1)}, u32[]{:S(2)}, u32[]{:S(2)}) %collective-permute-start) | collective-permute-done | bytes 917536 | tf_op jit(solution)/shard_map/ppermute | solution.py:100
  388.3 4.4 %shard_map.86 = bf16[512,14336]{1,0:T(8,128)(2,1)} custom-call(s32[16]{0:T(128)} %dynamic-slice_bitcast_fusion._, bf16[512,896]{1,0:T(8,128)(2,1)} %copy-done.7, f32[1,896]{1,0:T(1,128)} %broadcast_in_dim.83.norm_ref, f32[512,1]{1,0:T(8,128)} %copy.51.slope_ref, f32[512,1]{1,0:T(8,128)} %copy.52.shift_ref, ...), custom_call_target="tpu_custom_call", output_to_operand_aliasing={{}: (5, {})} | custom-call | flops 2752512 | bytes 1835008 | tf_op jit(solution)/shard_map/pallas_call | solution.py:74
  (178 shorter events, 159.9 us)
Async XLA Ops:
  18.7 11.5 %collective-permute-start.13 = (f32[896]{0:T(1024)S(1)}, f32[896]{0:T(1024)S(1)}, u32[]{:S(2)}, u32[]{:S(2)}) collective-permute-start(f32[896]{0:T(1024)S(1)} %get-tuple-element.25), channel_id=1, source_target_pairs={{0,24},{2,26},{4,28},{6,30},{8,10},{10,8},{12,14},{14,12},{16,18},... | collective-permute-start | bytes 10760 | tf_op jit(solution)/shard_map/ppermute | solution.py:100
  30.9 12.3 %collective-permute-start.5 = (f32[896]{0:T(1024)S(1)}, f32[896]{0:T(1024)S(1)}, u32[]{:S(2)}, u32[]{:S(2)}) collective-permute-start(f32[896]{0:T(1024)S(1)} %get-tuple-element.33), channel_id=1, source_target_pairs={{0,8},{2,10},{4,12},{6,14},{8,24},{10,26},{12,28},{14,30},{16,0},{... | collective-permute-start | bytes 10760 | tf_op jit(solution)/shard_map/ppermute | solution.py:100
  31.6 12.3 %collective-permute-start.6 = (f32[896]{0:T(1024)S(1)}, f32[896]{0:T(1024)S(1)}, u32[]{:S(2)}, u32[]{:S(2)}) collective-permute-start(f32[896]{0:T(1024)S(1)} %get-tuple-element.32), channel_id=1, source_target_pairs={{0,10},{2,8},{4,14},{6,12},{8,26},{10,24},{12,30},{14,28},{16,2},{... | collective-permute-start | bytes 10760 | tf_op jit(solution)/shard_map/ppermute | solution.py:100
  43.2 72.6 %collective-permute-start.47 = (bf16[512,896]{1,0:T(8,128)(2,1)}, bf16[512,896]{1,0:T(8,128)(2,1)S(1)}, u32[]{:S(2)}, u32[]{:S(2)}) collective-permute-start(bf16[512,896]{1,0:T(8,128)(2,1)} %shard_map.70), channel_id=1, source_target_pairs={{0,2},{2,0},{4,6},{6,4},{8,16},{10,18},{12,20},{14,22},{16,8},{18,... | collective-permute-start | bytes 2752520 | tf_op jit(solution)/shard_map/ppermute | solution.py:100
  56.9 11.6 %collective-permute-start.19 = (f32[1408]{0:T(1024)S(1)}, f32[1408]{0:T(1024)S(1)}, u32[]{:S(2)}, u32[]{:S(2)}) collective-permute-start(f32[1408]{0:T(1024)S(1)} %get-tuple-element.19), channel_id=1, source_target_pairs={{0,4},{2,6},{4,0},{6,2},{8,18},{10,16},{12,22},{14,20},{16,10},{18... | collective-permute-start | bytes 16904 | tf_op jit(solution)/shard_map/ppermute | solution.py:100
  76.3 13.9 %collective-permute-start.29 = (f32[1408]{0:T(1024)S(1)}, f32[1408]{0:T(1024)S(1)}, u32[]{:S(2)}, u32[]{:S(2)}) collective-permute-start(f32[1408]{0:T(1024)S(1)} %get-tuple-element.9), channel_id=1, source_target_pairs={{0,24},{2,26},{4,28},{6,30},{8,10},{10,8},{12,14},{14,12},{16,18},... | collective-permute-start | bytes 16904 | tf_op jit(solution)/shard_map/ppermute | solution.py:100
  78.4 17.0 %collective-permute-start.30 = (f32[1408]{0:T(1024)S(1)}, f32[1408]{0:T(1024)S(1)}, u32[]{:S(2)}, u32[]{:S(2)}) collective-permute-start(f32[1408]{0:T(1024)S(1)} %get-tuple-element.8), channel_id=1, source_target_pairs={{0,26},{2,24},{4,30},{6,28},{8,12},{10,14},{12,8},{14,10},{16,20},... | collective-permute-start | bytes 16904 | tf_op jit(solution)/shard_map/ppermute | solution.py:100
  79.4 20.1 %collective-permute-start.31 = (f32[1408]{0:T(1024)S(1)}, f32[1408]{0:T(1024)S(1)}, u32[]{:S(2)}, u32[]{:S(2)}) collective-permute-start(f32[1408]{0:T(1024)S(1)} %get-tuple-element.7), channel_id=1, source_target_pairs={{0,28},{2,30},{4,24},{6,26},{8,14},{10,12},{12,10},{14,8},{16,22},... | collective-permute-start | bytes 16904 | tf_op jit(solution)/shard_map/ppermute | solution.py:100
  82.0 29.8 %collective-permute-start.32 = (f32[1408]{0:T(1024)S(1)}, f32[1408]{0:T(1024)S(1)}, u32[]{:S(2)}, u32[]{:S(2)}) collective-permute-start(f32[1408]{0:T(1024)S(1)} %get-tuple-element.6), channel_id=1, source_target_pairs={{0,30},{2,28},{4,26},{6,24},{8,8},{10,10},{12,12},{14,14},{16,16},... | collective-permute-start | bytes 16904 | tf_op jit(solution)/shard_map/ppermute | solution.py:100
  90.2 32.5 %collective-permute-start.46 = (bf16[512,896]{1,0:T(8,128)(2,1)}, bf16[512,896]{1,0:T(8,128)(2,1)S(1)}, u32[]{:S(2)}, u32[]{:S(2)}) collective-permute-start(bf16[512,896]{1,0:T(8,128)(2,1)} %shard_map.69), channel_id=1, source_target_pairs={{0,4},{2,6},{4,0},{6,2},{8,18},{10,16},{12,22},{14,20},{16,10},{18... | collective-permute-start | bytes 2752520 | tf_op jit(solution)/shard_map/ppermute | solution.py:100
  95.3 36.1 %collective-permute-start.45 = (bf16[512,896]{1,0:T(8,128)(2,1)}, bf16[512,896]{1,0:T(8,128)(2,1)S(1)}, u32[]{:S(2)}, u32[]{:S(2)}) collective-permute-start(bf16[512,896]{1,0:T(8,128)(2,1)} %shard_map.68), channel_id=1, source_target_pairs={{0,6},{2,4},{4,2},{6,0},{8,20},{10,22},{12,16},{14,18},{16,12},{18... | collective-permute-start | bytes 2752520 | tf_op jit(solution)/shard_map/ppermute | solution.py:100
  99.6 35.9 %collective-permute-start.44 = (bf16[512,896]{1,0:T(8,128)(2,1)}, bf16[512,896]{1,0:T(8,128)(2,1)}, u32[]{:S(2)}, u32[]{:S(2)}) collective-permute-start(bf16[512,896]{1,0:T(8,128)(2,1)} %shard_map.67), channel_id=1, source_target_pairs={{0,0},{2,2},{4,4},{6,6},{8,22},{10,20},{12,18},{14,16},{16,14},{18... | collective-permute-start | bytes 2752520 | tf_op jit(solution)/shard_map/ppermute | solution.py:100
  111.8 114.9 %collective-permute-start.43 = (bf16[512,896]{1,0:T(8,128)(2,1)}, bf16[512,896]{1,0:T(8,128)(2,1)}, u32[]{:S(2)}, u32[]{:S(2)}) collective-permute-start(bf16[512,896]{1,0:T(8,128)(2,1)} %shard_map.66), channel_id=1, source_target_pairs={{0,8},{2,10},{4,12},{6,14},{8,24},{10,26},{12,28},{14,30},{16,0},{... | collective-permute-start | bytes 2752520 | tf_op jit(solution)/shard_map/ppermute | solution.py:100
  115.9 147.9 %collective-permute-start.42 = (bf16[512,896]{1,0:T(8,128)(2,1)}, bf16[512,896]{1,0:T(8,128)(2,1)}, u32[]{:S(2)}, u32[]{:S(2)}) collective-permute-start(bf16[512,896]{1,0:T(8,128)(2,1)} %shard_map.65), channel_id=1, source_target_pairs={{0,10},{2,8},{4,14},{6,12},{8,26},{10,24},{12,30},{14,28},{16,2},{... | collective-permute-start | bytes 2752520 | tf_op jit(solution)/shard_map/ppermute | solution.py:100
  122.6 148.0 %collective-permute-start.41 = (bf16[512,896]{1,0:T(8,128)(2,1)}, bf16[512,896]{1,0:T(8,128)(2,1)}, u32[]{:S(2)}, u32[]{:S(2)}) collective-permute-start(bf16[512,896]{1,0:T(8,128)(2,1)} %shard_map.64), channel_id=1, source_target_pairs={{0,16},{2,18},{4,20},{6,22},{8,0},{10,2},{12,4},{14,6},{16,24},{18... | collective-permute-start | bytes 2752520 | tf_op jit(solution)/shard_map/ppermute | solution.py:100
  131.5 144.5 %collective-permute-start.40 = (bf16[512,896]{1,0:T(8,128)(2,1)}, bf16[512,896]{1,0:T(8,128)(2,1)S(1)}, u32[]{:S(2)}, u32[]{:S(2)}) collective-permute-start(bf16[512,896]{1,0:T(8,128)(2,1)} %shard_map.63), channel_id=1, source_target_pairs={{0,18},{2,16},{4,22},{6,20},{8,2},{10,0},{12,6},{14,4},{16,26},{18... | collective-permute-start | bytes 2752520 | tf_op jit(solution)/shard_map/ppermute | solution.py:100
  135.5 146.6 %collective-permute-start.39 = (bf16[512,896]{1,0:T(8,128)(2,1)}, bf16[512,896]{1,0:T(8,128)(2,1)S(1)}, u32[]{:S(2)}, u32[]{:S(2)}) collective-permute-start(bf16[512,896]{1,0:T(8,128)(2,1)} %shard_map.62), channel_id=1, source_target_pairs={{0,20},{2,22},{4,16},{6,18},{8,4},{10,6},{12,0},{14,2},{16,28},{18... | collective-permute-start | bytes 2752520 | tf_op jit(solution)/shard_map/ppermute | solution.py:100
  226.8 63.0 %collective-permute-start.38 = (bf16[512,896]{1,0:T(8,128)(2,1)}, bf16[512,896]{1,0:T(8,128)(2,1)S(1)}, u32[]{:S(2)}, u32[]{:S(2)}) collective-permute-start(bf16[512,896]{1,0:T(8,128)(2,1)} %shard_map.61), channel_id=1, source_target_pairs={{0,22},{2,20},{4,18},{6,16},{8,6},{10,4},{12,2},{14,0},{16,30},{18... | collective-permute-start | bytes 2752520 | tf_op jit(solution)/shard_map/ppermute | solution.py:100
  263.8 30.7 %collective-permute-start.37 = (bf16[512,896]{1,0:T(8,128)(2,1)}, bf16[512,896]{1,0:T(8,128)(2,1)}, u32[]{:S(2)}, u32[]{:S(2)}) collective-permute-start(bf16[512,896]{1,0:T(8,128)(2,1)} %shard_map.60), channel_id=1, source_target_pairs={{0,24},{2,26},{4,28},{6,30},{8,10},{10,8},{12,14},{14,12},{16,18},... | collective-permute-start | bytes 2752520 | tf_op jit(solution)/shard_map/ppermute | solution.py:100
  270.6 93.0 %collective-permute-start.36 = (bf16[512,896]{1,0:T(8,128)(2,1)}, bf16[512,896]{1,0:T(8,128)(2,1)}, u32[]{:S(2)}, u32[]{:S(2)}) collective-permute-start(bf16[512,896]{1,0:T(8,128)(2,1)} %shard_map.59), channel_id=1, source_target_pairs={{0,26},{2,24},{4,30},{6,28},{8,12},{10,14},{12,8},{14,10},{16,20},... | collective-permute-start | bytes 2752520 | tf_op jit(solution)/shard_map/ppermute | solution.py:100
  275.9 92.0 %collective-permute-start.35 = (bf16[512,896]{1,0:T(8,128)(2,1)}, bf16[512,896]{1,0:T(8,128)(2,1)}, u32[]{:S(2)}, u32[]{:S(2)}) collective-permute-start(bf16[512,896]{1,0:T(8,128)(2,1)} %shard_map.58), channel_id=1, source_target_pairs={{0,28},{2,30},{4,24},{6,26},{8,14},{10,12},{12,10},{14,8},{16,22},... | collective-permute-start | bytes 2752520 | tf_op jit(solution)/shard_map/ppermute | solution.py:100
  282.1 90.2 %collective-permute-start.34 = (bf16[512,896]{1,0:T(8,128)(2,1)}, bf16[512,896]{1,0:T(8,128)(2,1)}, u32[]{:S(2)}, u32[]{:S(2)}) collective-permute-start(bf16[512,896]{1,0:T(8,128)(2,1)} %shard_map.57), channel_id=1, source_target_pairs={{0,30},{2,28},{4,26},{6,24},{8,8},{10,10},{12,12},{14,14},{16,16},... | collective-permute-start | bytes 2752520 | tf_op jit(solution)/shard_map/ppermute | solution.py:100
  289.7 86.9 %collective-permute-start.33 = (bf16[512,896]{1,0:T(8,128)(2,1)}, bf16[512,896]{1,0:T(8,128)(2,1)S(1)}, u32[]{:S(2)}, u32[]{:S(2)}) collective-permute-start(bf16[512,896]{1,0:T(8,128)(2,1)} %shard_map.56), channel_id=1, source_target_pairs={{0,12},{2,14},{4,8},{6,10},{8,28},{10,30},{12,24},{14,26},{16,4},{... | collective-permute-start | bytes 2752520 | tf_op jit(solution)/shard_map/ppermute | solution.py:100
  294.5 92.8 %collective-permute-start = (bf16[512,896]{1,0:T(8,128)(2,1)}, bf16[512,896]{1,0:T(8,128)(2,1)S(1)}, u32[]{:S(2)}, u32[]{:S(2)}) collective-permute-start(bf16[512,896]{1,0:T(8,128)(2,1)} %shard_map.55), channel_id=1, source_target_pairs={{0,14},{2,12},{4,10},{6,8},{8,30},{10,28},{12,26},{14,24},{16,6},{... | collective-permute-start | bytes 2752520 | tf_op jit(solution)/shard_map/ppermute | solution.py:100
  (33 other events, 306.3 us)

commit v2 on v0

v2 whole, which is shorter than its diff:
```python
import functools

import jax
import jax.numpy as jnp
import numpy as np
from jax import lax
from jax.experimental import pallas as pl
from jax.experimental.pallas import tpu as pltpu
from jax.sharding import PartitionSpec as P


gate_slope = 2.0
small_eps = 1e-06


def target(step, i, n, where=np.where):
    if n != 16:
        if n & (n - 1):
            return (i + step) % n
        return i ^ (step + n // 2) % n
    group, o = step // 4, step % 4
    place, seat = i // 4, i % 4
    if group in (0, 3):
        inner = (place == 1) | (place == 2)
        return where(inner == (group == 0), 12 - 4 * place + (seat ^ o), i ^ (o + 1) % 4)
    hop = (2 * place + 1) % 5 if group == 1 else (3 * place + 2) % 5
    return 4 * hop + (seat ^ o)


def prune_block(come, block, note, slope, shift, step, n, out, near):
    rows, cols = block.shape
    parts = 4 if rows % 64 == 0 else 1
    tile = rows // parts

    def body(come_ref, block_ref, note_ref, slope_ref, shift_ref, *rest):
        out_ref, wide_ref, done_ref, in_sem, out_sem = rest[-5:]
        at = pl.multiple_of(come_ref[step] * cols, 128)
        pieces = [pl.ds(p * tile, tile) for p in range(parts)]
        gets = []
        if not near:
            gets = [pltpu.make_async_copy(block_ref.at[s], wide_ref.at[s], in_sem.at[p]) for p, s in enumerate(pieces)]
        puts = [
            pltpu.make_async_copy(done_ref.at[s], out_ref.at[s, pl.ds(at, cols)], out_sem.at[p])
            for p, s in enumerate(pieces)
        ]
        for get in gets:
            get.start()
        norm = note_ref[:, rows:]
        for p, s in enumerate(pieces):
            if not near:
                gets[p].wait()
            wide = (block_ref if near else wide_ref)[s].astype(jnp.float32)
            share = jnp.clip(jnp.abs(wide) * norm * slope_ref[s] + shift_ref[s], 0.0, 1.0)
            done_ref[s] = (wide * share).astype(jnp.bfloat16)
            puts[p].start()
        for put in puts:
            put.wait()

    here, there = pl.BlockSpec(memory_space=pltpu.VMEM), pl.BlockSpec(memory_space=pl.ANY)
    in_specs = [pl.BlockSpec(memory_space=pltpu.SMEM), here if near else there, here, here, here]
    operands = [come, block, note, slope, shift]
    if out is not None:
        in_specs.append(there)
        operands.append(out)
    return pl.pallas_call(
        body,
        in_specs=in_specs,
        out_specs=there,
        scratch_shapes=[pltpu.VMEM((rows, cols), jnp.bfloat16)] * 2 + [pltpu.SemaphoreType.DMA((parts,))] * 2,
        out_shape=jax.ShapeDtypeStruct((rows, n * cols), jnp.bfloat16),
        input_output_aliases={} if out is None else {5: 0},
        cost_estimate=pl.CostEstimate(flops=6 * rows * cols, bytes_accessed=4 * rows * cols, transcendentals=0),
    )(*operands)


def per_device(n, n_mp, activations, weight, thresholds):
    ids = np.arange(n)
    plan = [target(k, ids, n) for k in range(n)]
    me = lax.axis_index("dp")
    tables = np.stack([np.stack(plan, 1), np.stack([np.argsort(p) for p in plan], 1)]).astype(np.int32)
    cols = weight.shape[1]
    rows = weight.shape[0] // n
    total_cols = cols * n * n_mp

    def send(x, step):
        return lax.ppermute(x, "dp", [(i, int(plan[step][i])) for i in range(n)])

    def take(source, step):
        return lax.dynamic_slice(source, (target(step, me, n, jnp.where) * rows, 0), (rows, cols))

    first = take(weight, 0)
    rest, _ = lax.optimization_barrier((weight, first))
    blocks = [first] + [take(rest, k) for k in range(1, n)]
    arrived = [send(blocks[k], k) for k in range(n)]

    to = lax.dynamic_index_in_dim(jnp.asarray(tables[0]), me, 0, keepdims=False)
    come = lax.dynamic_index_in_dim(jnp.asarray(tables[1]), me, 0, keepdims=False)
    partial_value = jnp.sum(jnp.square(activations.astype(jnp.float32)), axis=0)
    parts = jnp.take(partial_value.reshape(n, cols), to, axis=0)
    got = [send(parts[k], k) for k in range(n)]
    col_norm = jnp.sqrt(functools.reduce(jnp.add, got))
    row_part = jnp.sum(jnp.abs(weight.astype(jnp.float32)) * col_norm[None, :], axis=1).reshape(n, rows)
    notes = jnp.concatenate([jnp.take(row_part, to, axis=0), jnp.broadcast_to(col_norm, (n, cols))], axis=1)
    noted = [send(notes[k : k + 1], k) for k in range(n)]
    row_total = lax.psum(functools.reduce(jnp.add, [v[0, :rows] for v in noted]), "mp")
    row_mean = row_total / total_cols + small_eps
    slope = (gate_slope / row_mean)[:, None]
    shift = (0.5 - gate_slope * thresholds)[:, None]

    late = list(range(n // 2 - 2, n // 2))
    order = [v for v in range(n) if v not in late] + late
    if cols % 128 == 0 and rows % 128 == 0:
        out = None
        for k in order:
            near = k in order[-2:]
            out = prune_block(come, arrived[k], noted[k], slope, shift, k, n, out, near)
        return out
    out = jnp.zeros((rows, n * cols), jnp.bfloat16)
    for k in order:
        wide = arrived[k].astype(jnp.float32)
        share = jnp.clip(jnp.abs(wide) * noted[k][:, rows:] * slope + shift, 0.0, 1.0)
        out = lax.dynamic_update_slice(out, (wide * share).astype(jnp.bfloat16), (0, come[k] * cols))
    return out


def solution(mesh):
    placed = (P("dp", "mp"), P(None, ("mp", "dp")), P("dp"))
    n = mesh.shape["dp"]
    return jax.shard_map(
        functools.partial(per_device, n, mesh.shape["mp"]),
        mesh=mesh,
        in_specs=placed,
        out_specs=P("dp", "mp"),
        check_vma=False,
    )
```

time: 434 us -> 394 us (0.908)
  blocking collectives: 353 us -> 5.11 us
  waiting for transfers between devices: 0.01 us -> 167 us
  starting transfers between devices: 7.46 us -> 132 us
  Pallas kernels: 0 us -> 52.2 us
  local copies, waits for them, and re-layouts: 40.6 us -> 14 us
  other arithmetic: 31.4 us -> 21.2 us
    psum x2 -> x1, blocking collectives: 353 us -> 5.11 us  [per_device(): lax.psum(functools.reduce(jnp.add, [v[0, :rows] for v in noted]), 'mp')]
    ppermute x0 -> x48, waiting for transfers between devices: none -> 167 us  [send(): return lax.ppermute(x, 'dp', [(i, int(plan[step][i])) for i in range(n)])]
    ppermute x0 -> x48, starting transfers between devices: none -> 132 us  [send(): return lax.ppermute(x, 'dp', [(i, int(plan[step][i])) for i in range(n)])]
    pallas_call x0 -> x16, Pallas kernels: none -> 52.2 us  [prune_block(): pl.pallas_call(body, in_specs=in_specs, out_specs=there, scratch_shapes=[...]
    all_to_all x1 -> x0, local copies, waits for them, and re-layouts: 20.7 us -> none  [per_device(): lax.all_to_all(weight, 'dp', split_axis=0, concat_axis=1, tiled=True)]
    convert_element_type x1 -> x0, local copies, waits for them, and re-layouts: 19.9 us -> none  [soft_prune(): return (wide * kept_share).astype(jnp.bfloat16)]
    convert_element_type x1 -> x0, other arithmetic: 16 us -> none  [soft_prune(): return (wide * kept_share).astype(jnp.bfloat16)]
    dynamic_slice x0 -> x2, local copies, waits for them, and re-layouts: none -> 8.6 us  [take(): lax.dynamic_slice(source, (target(step, me, n, jnp.where) * rows, 0), (ro...]
  transfers between devices with their start and end apart: 1 -> 48, of which waited for: 0 -> 12; matrix products, arithmetic and copies ran while one was open for 2% -> 6% of each run, Pallas kernels for 0% -> 13%
where the time goes in v2:
time: 394 us; the launch traced here: 392 us
  waiting for transfers between devices  167 us (42%)
  starting transfers between devices  132 us (34%)
  Pallas kernels  52.2 us (13%)
  other arithmetic  21.2 us (5%)
  local copies, waits for them, and re-layouts  14 us (4%)
  blocking collectives  5.11 us (1%)
    ppermute x48, waiting for transfers between devices, send(): return lax.ppermute(x, 'dp', [(i, int(plan[step][i])) for i in range(n)])  167 us
    ppermute x48, starting transfers between devices, send(): return lax.ppermute(x, 'dp', [(i, int(plan[step][i])) for i in range(n)])  132 us
    pallas_call x16, Pallas kernels, prune_block(): pl.pallas_call(body, in_specs=in_specs, out_specs=there, scratch_shapes=[...  52.2 us
    reduce_sum x1, other arithmetic, per_device(): jnp.sum(jnp.abs(weight.astype(jnp.float32)) * col_norm[None, :], axis=1)  11.1 us
    dynamic_slice x2, local copies, waits for them, and re-layouts, take(): lax.dynamic_slice(source, (target(step, me, n, jnp.where) * rows, 0), (ro...  8.6 us
    reduce_sum x1, other arithmetic, per_device(): partial_value = jnp.sum(jnp.square(activations.astype(jnp.float32)), axis=0)  8.52 us
  transfers between devices with their start and end apart: 48, of which 12 were waited for; matrix products, arithmetic and copies ran while one was open for 6% of the time, Pallas kernels for 13%

profile of v2, /device:TPU:0, one launch (start us, length us, event | category | flops | bytes accessed | tf_op | source)
XLA Modules:
  0.0 392.1 jit_solution(2275705305591589992)
XLA Ops:
  1.4 8.5 %multiply_reduce_fusion.1 = f32[14336]{0:T(1024)S(1)} fusion(bf16[512,14336]{1,0:T(8,128)(2,1)} %param.5), kind=kLoop, calls=%fused_computation.3 | loop fusion | flops 22005760 | bytes 14737408 | tf_op jit(solution)/shard_map/reduce_sum | solution.py:98
  13.8 4.6 %collective-permute-start.16 = (f32[896]{0:T(1024)S(1)}, f32[896]{0:T(1024)S(1)}, u32[]{:S(2)}, u32[]{:S(2)}) collective-permute-start(f32[896]{0:T(1024)S(1)} %get-tuple-element.8), channel_id=1, source_target_pairs={{0,30},{2,28},{4,26},{6,24},{8,8},{10,10},{12,12},{14,14},{16,16},... | collective-permute-start | bytes 10760 | tf_op jit(solution)/shard_map/ppermute | solution.py:86
  19.7 3.9 collective-permute-start.14
  23.8 4.2 %collective-permute-start.11 = (f32[896]{0:T(1024)S(1)}, f32[896]{0:T(1024)S(1)}, u32[]{:S(2)}, u32[]{:S(2)}) collective-permute-start(f32[896]{0:T(1024)S(1)} %get-tuple-element.13), channel_id=1, source_target_pairs={{0,20},{2,22},{4,16},{6,18},{8,4},{10,6},{12,0},{14,2},{16,28},{18... | collective-permute-start | bytes 10760 | tf_op jit(solution)/shard_map/ppermute | solution.py:86
  38.2 11.1 %multiply_reduce_fusion = f32[8192]{0:T(1024)S(1)} fusion(bf16[8192,896]{1,0:T(8,128)(2,1)} %param.6, f32[896]{0:T(1024)S(1)} %add_sqrt_fusion), kind=kLoop, calls=%fused_computation.2 | loop fusion | flops 29351936 | bytes 14716416 | tf_op jit(solution)/shard_map/reduce_sum | solution.py:102
  50.2 5.4 %collective-permute-start.32 = (f32[1,1408]{1,0:T(1,128)S(1)}, f32[1,1408]{1,0:T(1,128)S(1)}, u32[]{:S(2)}, u32[]{:S(2)}) collective-permute-start(f32[1,1408]{1,0:T(1,128)S(1)} %get-tuple-element.39), channel_id=1, source_target_pairs={{0,30},{2,28},{4,26},{6,24},{8,8},{10,10},{12,12},{14,14},{16,16},... | collective-permute-start | bytes 16904 | tf_op jit(solution)/shard_map/ppermute | solution.py:86
  60.6 5.6 %collective-permute-start.28 = (f32[1,1408]{1,0:T(1,128)S(1)}, f32[1,1408]{1,0:T(1,128)S(1)}, u32[]{:S(2)}, u32[]{:S(2)}) collective-permute-start(f32[1,1408]{1,0:T(1,128)S(1)} %get-tuple-element.43), channel_id=1, source_target_pairs={{0,22},{2,20},{4,18},{6,16},{8,6},{10,4},{12,2},{14,0},{16,30},{18... | collective-permute-start | bytes 16904 | tf_op jit(solution)/shard_map/ppermute | solution.py:86
  76.5 3.9 collective-permute-start.17
  80.4 7.4 %constant_dynamic-slice_fusion = (bf16[512,896]{1,0:T(8,128)(2,1)S(1)}, bf16[512,896]{1,0:T(8,128)(2,1)S(1)}, bf16[512,896]{1,0:T(8,128)(2,1)S(1)}, bf16[512,896...) fusion(bf16[8192,896]{1,0:T(8,128)(2,1)} %param.6, ...), kind=kLoop, calls=%fused_computation.7 | loop fusion | bytes 27525180 | tf_op jit(solution)/shard_map/dynamic_slice | solution.py:89
  93.4 17.6 %collective-permute-done.46.block_ref = bf16[512,896]{1,0:T(8,128)(2,1)S(1)} collective-permute-done((bf16[512,896]{1,0:T(8,128)(2,1)S(1)}, bf16[512,896]{1,0:T(8,128)(2,1)S(1)}, u32[]{:S(2)}, u32[]{:S(2)}) %collective-permute-start.46) | collective-permute-done | bytes 917536 | tf_op jit(solution)/shard_map/ppermute | solution.py:86
  111.1 17.4 %collective-permute-done.45.block_ref = bf16[512,896]{1,0:T(8,128)(2,1)S(1)} collective-permute-done((bf16[512,896]{1,0:T(8,128)(2,1)S(1)}, bf16[512,896]{1,0:T(8,128)(2,1)S(1)}, u32[]{:S(2)}, u32[]{:S(2)}) %collective-permute-start.45) | collective-permute-done | bytes 917536 | tf_op jit(solution)/shard_map/ppermute | solution.py:86
  129.5 59.6 %collective-permute-start.39 = (bf16[512,896]{1,0:T(8,128)(2,1)S(1)}, bf16[512,896]{1,0:T(8,128)(2,1)S(1)}, u32[]{:S(2)}, u32[]{:S(2)}) collective-permute-start(bf16[512,896]{1,0:T(8,128)(2,1)S(1)} %get-tuple-element.30), channel_id=1, source_target_pairs={{0,20},{2,22},{4,16},{6,18},{8,4},{10,6},{12,0},{14,2},{16,28},{18... | collective-permute-start | bytes 2752520 | tf_op jit(solution)/shard_map/ppermute | solution.py:86
  189.2 38.8 %collective-permute-done.43.block_ref = bf16[512,896]{1,0:T(8,128)(2,1)S(1)} collective-permute-done((bf16[512,896]{1,0:T(8,128)(2,1)S(1)}, bf16[512,896]{1,0:T(8,128)(2,1)S(1)}, u32[]{:S(2)}, u32[]{:S(2)}) %collective-permute-start.43) | collective-permute-done | bytes 917536 | tf_op jit(solution)/shard_map/ppermute | solution.py:86
  228.0 37.6 %collective-permute-done.42.block_ref = bf16[512,896]{1,0:T(8,128)(2,1)S(1)} collective-permute-done((bf16[512,896]{1,0:T(8,128)(2,1)S(1)}, bf16[512,896]{1,0:T(8,128)(2,1)S(1)}, u32[]{:S(2)}, u32[]{:S(2)}) %collective-permute-start.42) | collective-permute-done | bytes 917536 | tf_op jit(solution)/shard_map/ppermute | solution.py:86
  276.7 14.0 %collective-permute-done.37.block_ref = bf16[512,896]{1,0:T(8,128)(2,1)S(1)} collective-permute-done((bf16[512,896]{1,0:T(8,128)(2,1)S(1)}, bf16[512,896]{1,0:T(8,128)(2,1)S(1)}, u32[]{:S(2)}, u32[]{:S(2)}) %collective-permute-start.37) | collective-permute-done | bytes 917536 | tf_op jit(solution)/shard_map/ppermute | solution.py:86
  293.9 5.1 %psum.7 = f32[512]{0:T(512)S(1)} all-reduce(f32[512]{0:T(512)S(1)} %bitcast.13), channel_id=1, replica_groups=mesh['dp'=16,'mp'=2] {'mp'}, use_global_device_ids=true, to_apply=%region_2.3 | all-reduce | flops 512 | bytes 4096 | tf_op jit(solution)/shard_map/psum | solution.py:105
  303.3 3.4 shard_map.56.rest_0_
  306.8 3.4 shard_map.57.rest_0_
  323.6 3.4 shard_map.62.rest_0_
  326.9 3.4 shard_map.63.rest_0_
  337.0 3.4 shard_map.66.rest_0_
  343.8 6.0 %collective-permute-done.34.block_ref = bf16[512,896]{1,0:T(8,128)(2,1)} collective-permute-done((bf16[512,896]{1,0:T(8,128)(2,1)}, bf16[512,896]{1,0:T(8,128)(2,1)}, u32[]{:S(2)}, u32[]{:S(2)}) %collective-permute-start.34) | collective-permute-done | bytes 917536 | tf_op jit(solution)/shard_map/ppermute | solution.py:86
  353.2 16.5 %collective-permute-done.33.block_ref = bf16[512,896]{1,0:T(8,128)(2,1)} collective-permute-done((bf16[512,896]{1,0:T(8,128)(2,1)}, bf16[512,896]{1,0:T(8,128)(2,1)}, u32[]{:S(2)}, u32[]{:S(2)}) %collective-permute-start.33) | collective-permute-done | bytes 917536 | tf_op jit(solution)/shard_map/ppermute | solution.py:86
  372.3 17.0 %collective-permute-done.block_ref = bf16[512,896]{1,0:T(8,128)(2,1)} collective-permute-done((bf16[512,896]{1,0:T(8,128)(2,1)S(1)}, bf16[512,896]{1,0:T(8,128)(2,1)}, u32[]{:S(2)}, u32[]{:S(2)}) %collective-permute-start) | collective-permute-done | bytes 917536 | tf_op jit(solution)/shard_map/ppermute | solution.py:86
  (169 shorter events, 90.2 us)
Async XLA Ops:
  10.8 13.0 %collective-permute-start.2 = (f32[896]{0:T(1024)S(1)}, f32[896]{0:T(1024)S(1)}, u32[]{:S(2)}, u32[]{:S(2)}) collective-permute-start(f32[896]{0:T(1024)S(1)} %get-tuple-element.7), channel_id=1, source_target_pairs={{0,4},{2,6},{4,0},{6,2},{8,18},{10,16},{12,22},{14,20},{16,10},{18... | collective-permute-start | bytes 10760 | tf_op jit(solution)/shard_map/ppermute | solution.py:86
  13.8 10.0 %collective-permute-start.16 = (f32[896]{0:T(1024)S(1)}, f32[896]{0:T(1024)S(1)}, u32[]{:S(2)}, u32[]{:S(2)}) collective-permute-start(f32[896]{0:T(1024)S(1)} %get-tuple-element.8), channel_id=1, source_target_pairs={{0,30},{2,28},{4,26},{6,24},{8,8},{10,10},{12,12},{14,14},{16,16},... | collective-permute-start | bytes 10760 | tf_op jit(solution)/shard_map/ppermute | solution.py:86
  37.3 55.5 %collective-permute-start.47 = (bf16[512,896]{1,0:T(8,128)(2,1)S(1)}, bf16[512,896]{1,0:T(8,128)(2,1)S(1)}, u32[]{:S(2)}, u32[]{:S(2)}) collective-permute-start(bf16[512,896]{1,0:T(8,128)(2,1)S(1)} %constant_dynamic-slice_fusion.16), channel_id=1, source_target_pairs={{0,2},{2,0},{4,6},{6,4},{8,16},{10,18},{12,20},{14,22},{16,8},{18,... | collective-permute-start | bytes 2752520 | tf_op jit(solution)/shard_map/ppermute | solution.py:86
  50.2 10.4 %collective-permute-start.32 = (f32[1,1408]{1,0:T(1,128)S(1)}, f32[1,1408]{1,0:T(1,128)S(1)}, u32[]{:S(2)}, u32[]{:S(2)}) collective-permute-start(f32[1,1408]{1,0:T(1,128)S(1)} %get-tuple-element.39), channel_id=1, source_target_pairs={{0,30},{2,28},{4,26},{6,24},{8,8},{10,10},{12,12},{14,14},{16,16},... | collective-permute-start | bytes 16904 | tf_op jit(solution)/shard_map/ppermute | solution.py:86
  55.7 10.5 %collective-permute-start.31 = (f32[1,1408]{1,0:T(1,128)S(1)}, f32[1,1408]{1,0:T(1,128)S(1)}, u32[]{:S(2)}, u32[]{:S(2)}) collective-permute-start(f32[1,1408]{1,0:T(1,128)S(1)} %get-tuple-element.40), channel_id=1, source_target_pairs={{0,28},{2,30},{4,24},{6,26},{8,14},{10,12},{12,10},{14,8},{16,22},... | collective-permute-start | bytes 16904 | tf_op jit(solution)/shard_map/ppermute | solution.py:86
  73.3 14.4 %collective-permute-start.21 = (f32[1,1408]{1,0:T(1,128)S(1)}, f32[1,1408]{1,0:T(1,128)S(1)}, u32[]{:S(2)}, u32[]{:S(2)}) collective-permute-start(f32[1,1408]{1,0:T(1,128)S(1)} %get-tuple-element.50), channel_id=1, source_target_pairs={{0,0},{2,2},{4,4},{6,6},{8,22},{10,20},{12,18},{14,16},{16,14},{18... | collective-permute-start | bytes 16904 | tf_op jit(solution)/shard_map/ppermute | solution.py:86
  75.1 13.5 %collective-permute-start.20 = (f32[1,1408]{1,0:T(1,128)S(1)}, f32[1,1408]{1,0:T(1,128)S(1)}, u32[]{:S(2)}, u32[]{:S(2)}) collective-permute-start(f32[1,1408]{1,0:T(1,128)S(1)} %get-tuple-element.51), channel_id=1, source_target_pairs={{0,6},{2,4},{4,2},{6,0},{8,20},{10,22},{12,16},{14,18},{16,12},{18... | collective-permute-start | bytes 16904 | tf_op jit(solution)/shard_map/ppermute | solution.py:86
  75.4 13.6 %collective-permute-start.19 = (f32[1,1408]{1,0:T(1,128)S(1)}, f32[1,1408]{1,0:T(1,128)S(1)}, u32[]{:S(2)}, u32[]{:S(2)}) collective-permute-start(f32[1,1408]{1,0:T(1,128)S(1)} %get-tuple-element.52), channel_id=1, source_target_pairs={{0,4},{2,6},{4,0},{6,2},{8,18},{10,16},{12,22},{14,20},{16,10},{18... | collective-permute-start | bytes 16904 | tf_op jit(solution)/shard_map/ppermute | solution.py:86
  76.5 13.3 %collective-permute-start.17 = (f32[1,1408]{1,0:T(1,128)S(1)}, f32[1,1408]{1,0:T(1,128)S(1)}, u32[]{:S(2)}, u32[]{:S(2)}) collective-permute-start(f32[1,1408]{1,0:T(1,128)S(1)} %get-tuple-element.53), channel_id=1, source_target_pairs={{0,14},{2,12},{4,10},{6,8},{8,30},{10,28},{12,26},{14,24},{16,6},{... | collective-permute-start | bytes 16904 | tf_op jit(solution)/shard_map/ppermute | solution.py:86
  87.8 23.3 %collective-permute-start.46 = (bf16[512,896]{1,0:T(8,128)(2,1)S(1)}, bf16[512,896]{1,0:T(8,128)(2,1)S(1)}, u32[]{:S(2)}, u32[]{:S(2)}) collective-permute-start(bf16[512,896]{1,0:T(8,128)(2,1)S(1)} %get-tuple-element.23), channel_id=1, source_target_pairs={{0,4},{2,6},{4,0},{6,2},{8,18},{10,16},{12,22},{14,20},{16,10},{18... | collective-permute-start | bytes 2752520 | tf_op jit(solution)/shard_map/ppermute | solution.py:86
  88.7 39.8 %collective-permute-start.45 = (bf16[512,896]{1,0:T(8,128)(2,1)S(1)}, bf16[512,896]{1,0:T(8,128)(2,1)S(1)}, u32[]{:S(2)}, u32[]{:S(2)}) collective-permute-start(bf16[512,896]{1,0:T(8,128)(2,1)S(1)} %get-tuple-element.24), channel_id=1, source_target_pairs={{0,6},{2,4},{4,2},{6,0},{8,20},{10,22},{12,16},{14,18},{16,12},{18... | collective-permute-start | bytes 2752520 | tf_op jit(solution)/shard_map/ppermute | solution.py:86
  89.0 40.5 %collective-permute-start.44 = (bf16[512,896]{1,0:T(8,128)(2,1)S(1)}, bf16[512,896]{1,0:T(8,128)(2,1)S(1)}, u32[]{:S(2)}, u32[]{:S(2)}) collective-permute-start(bf16[512,896]{1,0:T(8,128)(2,1)S(1)} %get-tuple-element.25), channel_id=1, source_target_pairs={{0,0},{2,2},{4,4},{6,6},{8,22},{10,20},{12,18},{14,16},{16,14},{18... | collective-permute-start | bytes 2752520 | tf_op jit(solution)/shard_map/ppermute | solution.py:86
  89.8 138.2 %collective-permute-start.43 = (bf16[512,896]{1,0:T(8,128)(2,1)S(1)}, bf16[512,896]{1,0:T(8,128)(2,1)S(1)}, u32[]{:S(2)}, u32[]{:S(2)}) collective-permute-start(bf16[512,896]{1,0:T(8,128)(2,1)S(1)} %get-tuple-element.26), channel_id=1, source_target_pairs={{0,8},{2,10},{4,12},{6,14},{8,24},{10,26},{12,28},{14,30},{16,0},{... | collective-permute-start | bytes 2752520 | tf_op jit(solution)/shard_map/ppermute | solution.py:86
  92.8 172.8 %collective-permute-start.42 = (bf16[512,896]{1,0:T(8,128)(2,1)S(1)}, bf16[512,896]{1,0:T(8,128)(2,1)S(1)}, u32[]{:S(2)}, u32[]{:S(2)}) collective-permute-start(bf16[512,896]{1,0:T(8,128)(2,1)S(1)} %get-tuple-element.27), channel_id=1, source_target_pairs={{0,10},{2,8},{4,14},{6,12},{8,26},{10,24},{12,30},{14,28},{16,2},{... | collective-permute-start | bytes 2752520 | tf_op jit(solution)/shard_map/ppermute | solution.py:86
  111.1 156.8 %collective-permute-start.41 = (bf16[512,896]{1,0:T(8,128)(2,1)S(1)}, bf16[512,896]{1,0:T(8,128)(2,1)S(1)}, u32[]{:S(2)}, u32[]{:S(2)}) collective-permute-start(bf16[512,896]{1,0:T(8,128)(2,1)S(1)} %get-tuple-element.28), channel_id=1, source_target_pairs={{0,16},{2,18},{4,20},{6,22},{8,0},{10,2},{12,4},{14,6},{16,24},{18... | collective-permute-start | bytes 2752520 | tf_op jit(solution)/shard_map/ppermute | solution.py:86
  128.4 141.0 %collective-permute-start.40 = (bf16[512,896]{1,0:T(8,128)(2,1)S(1)}, bf16[512,896]{1,0:T(8,128)(2,1)S(1)}, u32[]{:S(2)}, u32[]{:S(2)}) collective-permute-start(bf16[512,896]{1,0:T(8,128)(2,1)S(1)} %get-tuple-element.29), channel_id=1, source_target_pairs={{0,18},{2,16},{4,22},{6,20},{8,2},{10,0},{12,6},{14,4},{16,26},{18... | collective-permute-start | bytes 2752520 | tf_op jit(solution)/shard_map/ppermute | solution.py:86
  129.5 142.7 %collective-permute-start.39 = (bf16[512,896]{1,0:T(8,128)(2,1)S(1)}, bf16[512,896]{1,0:T(8,128)(2,1)S(1)}, u32[]{:S(2)}, u32[]{:S(2)}) collective-permute-start(bf16[512,896]{1,0:T(8,128)(2,1)S(1)} %get-tuple-element.30), channel_id=1, source_target_pairs={{0,20},{2,22},{4,16},{6,18},{8,4},{10,6},{12,0},{14,2},{16,28},{18... | collective-permute-start | bytes 2752520 | tf_op jit(solution)/shard_map/ppermute | solution.py:86
  228.0 47.6 %collective-permute-start.38 = (bf16[512,896]{1,0:T(8,128)(2,1)S(1)}, bf16[512,896]{1,0:T(8,128)(2,1)S(1)}, u32[]{:S(2)}, u32[]{:S(2)}) collective-permute-start(bf16[512,896]{1,0:T(8,128)(2,1)S(1)} %get-tuple-element.31), channel_id=1, source_target_pairs={{0,22},{2,20},{4,18},{6,16},{8,6},{10,4},{12,2},{14,0},{16,30},{18... | collective-permute-start | bytes 2752520 | tf_op jit(solution)/shard_map/ppermute | solution.py:86
  265.6 25.1 %collective-permute-start.37 = (bf16[512,896]{1,0:T(8,128)(2,1)S(1)}, bf16[512,896]{1,0:T(8,128)(2,1)S(1)}, u32[]{:S(2)}, u32[]{:S(2)}) collective-permute-start(bf16[512,896]{1,0:T(8,128)(2,1)S(1)} %get-tuple-element.32), channel_id=1, source_target_pairs={{0,24},{2,26},{4,28},{6,30},{8,10},{10,8},{12,14},{14,12},{16,18},... | collective-permute-start | bytes 2752520 | tf_op jit(solution)/shard_map/ppermute | solution.py:86
  267.9 69.2 %collective-permute-start.36 = (bf16[512,896]{1,0:T(8,128)(2,1)}, bf16[512,896]{1,0:T(8,128)(2,1)}, u32[]{:S(2)}, u32[]{:S(2)}) collective-permute-start(bf16[512,896]{1,0:T(8,128)(2,1)} %get-tuple-element.33), channel_id=1, source_target_pairs={{0,26},{2,24},{4,30},{6,28},{8,12},{10,14},{12,8},{14,10},{16,20},... | collective-permute-start | bytes 2752520 | tf_op jit(solution)/shard_map/ppermute | solution.py:86
  269.4 71.0 %collective-permute-start.35 = (bf16[512,896]{1,0:T(8,128)(2,1)}, bf16[512,896]{1,0:T(8,128)(2,1)}, u32[]{:S(2)}, u32[]{:S(2)}) collective-permute-start(bf16[512,896]{1,0:T(8,128)(2,1)} %get-tuple-element.34), channel_id=1, source_target_pairs={{0,28},{2,30},{4,24},{6,26},{8,14},{10,12},{12,10},{14,8},{16,22},... | collective-permute-start | bytes 2752520 | tf_op jit(solution)/shard_map/ppermute | solution.py:86
  272.2 77.6 %collective-permute-start.34 = (bf16[512,896]{1,0:T(8,128)(2,1)}, bf16[512,896]{1,0:T(8,128)(2,1)}, u32[]{:S(2)}, u32[]{:S(2)}) collective-permute-start(bf16[512,896]{1,0:T(8,128)(2,1)} %get-tuple-element.35), channel_id=1, source_target_pairs={{0,30},{2,28},{4,26},{6,24},{8,8},{10,10},{12,12},{14,14},{16,16},... | collective-permute-start | bytes 2752520 | tf_op jit(solution)/shard_map/ppermute | solution.py:86
  275.5 94.2 %collective-permute-start.33 = (bf16[512,896]{1,0:T(8,128)(2,1)}, bf16[512,896]{1,0:T(8,128)(2,1)}, u32[]{:S(2)}, u32[]{:S(2)}) collective-permute-start(bf16[512,896]{1,0:T(8,128)(2,1)} %get-tuple-element.36), channel_id=1, source_target_pairs={{0,12},{2,14},{4,8},{6,10},{8,28},{10,30},{12,24},{14,26},{16,4},{... | collective-permute-start | bytes 2752520 | tf_op jit(solution)/shard_map/ppermute | solution.py:86
  290.7 98.6 %collective-permute-start = (bf16[512,896]{1,0:T(8,128)(2,1)S(1)}, bf16[512,896]{1,0:T(8,128)(2,1)}, u32[]{:S(2)}, u32[]{:S(2)}) collective-permute-start(bf16[512,896]{1,0:T(8,128)(2,1)S(1)} %get-tuple-element.37), channel_id=1, source_target_pairs={{0,14},{2,12},{4,10},{6,8},{8,30},{10,28},{12,26},{14,24},{16,6},{... | collective-permute-start | bytes 2752520 | tf_op jit(solution)/shard_map/ppermute | solution.py:86
  (52 other events, 4951.2 us)

commit v3 on v2

v3 whole, which is shorter than its diff:
```python
import functools

import jax
import jax.numpy as jnp
import numpy as np
from jax import lax
from jax.experimental import pallas as pl
from jax.experimental.pallas import tpu as pltpu
from jax.sharding import PartitionSpec as P


gate_slope = 2.0
small_eps = 1e-06


def target(step, i, n, where=np.where):
    if n != 16:
        if n & (n - 1):
            return (i + step) % n
        return i ^ (step + n // 2) % n
    group, o = step // 4, step % 4
    place, seat = i >> 2, i & 3
    if group in (1, 3):
        inner = (place == 1) | (place == 2)
        return where(inner == (group == 1), 12 - 4 * place + (seat ^ o), i ^ ((o + 1) % 4))
    hop = ((place & 1) << 1) + ((place >> 1) ^ 1) if group == 0 else (((place & 1) ^ 1) << 1) + (place >> 1)
    return 4 * hop + (seat ^ o)


def pieces_of(n, rows):
    cut = rows // 4
    pieces = []
    for step in range(n):
        if rows % 64 or step not in (0, n // 2 - 1):
            pieces.append((step, 0, rows))
        else:
            split = cut if step == 0 else rows - cut
            pieces += [(step, 0, split), (step, split, rows - split)]
    return pieces


def prune_block(come, block, note, slope, shift, step, top, n, out, near):
    rows, cols = slope.shape[0], block.shape[1]
    size = block.shape[0]
    parts = max(size // 128, 1)
    tile = size // parts

    def body(come_ref, block_ref, note_ref, slope_ref, shift_ref, *rest):
        out_ref, wide_ref, done_ref, in_sem, out_sem = rest[-5:]
        at = pl.multiple_of(come_ref[step] * cols, 128)
        here = [pl.ds(p * tile, tile) for p in range(parts)]
        there = [pl.ds(top + p * tile, tile) for p in range(parts)]
        gets = []
        if not near:
            gets = [pltpu.make_async_copy(block_ref.at[s], wide_ref.at[s], in_sem.at[p]) for p, s in enumerate(here)]
        for get in gets:
            get.start()
        norm = note_ref[:, rows:]
        puts = []
        for p, (s, d) in enumerate(zip(here, there)):
            if not near:
                gets[p].wait()
            wide = (block_ref if near else wide_ref)[s].astype(jnp.float32)
            share = jnp.clip(jnp.abs(wide) * norm * slope_ref[d] + shift_ref[d], 0.0, 1.0)
            done_ref[s] = (wide * share).astype(jnp.bfloat16)
            puts.append(pltpu.make_async_copy(done_ref.at[s], out_ref.at[d, pl.ds(at, cols)], out_sem.at[p]))
            puts[-1].start()
        for put in puts:
            put.wait()

    here, there = pl.BlockSpec(memory_space=pltpu.VMEM), pl.BlockSpec(memory_space=pl.ANY)
    in_specs = [pl.BlockSpec(memory_space=pltpu.SMEM), here if near else there, here, here, here]
    operands = [come, block, note, slope, shift]
    if out is not None:
        in_specs.append(there)
        operands.append(out)
    return pl.pallas_call(
        body,
        in_specs=in_specs,
        out_specs=there,
        scratch_shapes=[pltpu.VMEM((size, cols), jnp.bfloat16)] * 2 + [pltpu.SemaphoreType.DMA((parts,))] * 2,
        out_shape=jax.ShapeDtypeStruct((rows, n * cols), jnp.bfloat16),
        input_output_aliases={} if out is None else {5: 0},
        cost_estimate=pl.CostEstimate(flops=6 * size * cols, bytes_accessed=4 * size * cols, transcendentals=0),
    )(*operands)


def per_device(n, n_mp, activations, weight, thresholds):
    ids = np.arange(n)
    plan = [target(k, ids, n) for k in range(n)]
    me = lax.axis_index("dp")
    tables = np.stack([np.stack(plan, 1), np.stack([np.argsort(p) for p in plan], 1)]).astype(np.int32)
    cols = weight.shape[1]
    rows = weight.shape[0] // n
    total_cols = cols * n * n_mp

    pieces = pieces_of(n, rows)

    def send(x, step):
        return lax.ppermute(x, "dp", [(i, int(plan[step][i])) for i in range(n)])

    def take(source, step, top, size):
        return lax.dynamic_slice(source, (target(step, me, n, jnp.where) * rows + top, 0), (size, cols))

    blocks, source = [], weight
    for piece in pieces:
        blocks.append(take(source, *piece))
        if len(blocks) <= 2:
            source, _ = lax.optimization_barrier((source, blocks[-1]))
    arrived = [send(block, step) for block, (step, _, _) in zip(blocks, pieces)]

    to = lax.dynamic_index_in_dim(jnp.asarray(tables[0]), me, 0, keepdims=False)
    come = lax.dynamic_index_in_dim(jnp.asarray(tables[1]), me, 0, keepdims=False)
    partial_value = jnp.sum(jnp.square(activations.astype(jnp.float32)), axis=0)
    parts = jnp.take(partial_value.reshape(n, cols), to, axis=0)
    got = [send(parts[k], k) for k in range(n)]
    col_norm = jnp.sqrt(functools.reduce(jnp.add, got))
    row_part = jnp.sum(jnp.abs(weight.astype(jnp.float32)) * col_norm[None, :], axis=1).reshape(n, rows)
    notes = jnp.concatenate([jnp.take(row_part, to, axis=0), jnp.broadcast_to(col_norm, (n, cols))], axis=1)
    noted = [send(notes[k : k + 1], k) for k in range(n)]
    row_total = lax.psum(functools.reduce(jnp.add, [v[0, :rows] for v in noted]), "mp")
    row_mean = row_total / total_cols + small_eps
    slope = (gate_slope / row_mean)[:, None]
    shift = (0.5 - gate_slope * thresholds)[:, None]

    late = [i for i, (step, _, _) in enumerate(pieces) if step in (n // 2 - 2, n // 2 - 1)]
    order = [i for i in range(len(pieces)) if i not in late] + late
    if cols % 128 == 0 and rows % 128 == 0:
        out = None
        for i in order:
            step, top, _ = pieces[i]
            near = i in order[-2:]
            out = prune_block(come, arrived[i], noted[step], slope, shift, step, top, n, out, near)
        return out
    out = jnp.zeros((rows, n * cols), jnp.bfloat16)
    for i in order:
        step, top, size = pieces[i]
        wide = arrived[i].astype(jnp.float32)
        ours = slice(top, top + size)
        share = jnp.clip(jnp.abs(wide) * noted[step][:, rows:] * slope[ours] + shift[ours], 0.0, 1.0)
        out = lax.dynamic_update_slice(out, (wide * share).astype(jnp.bfloat16), (top, come[step] * cols))
    return out


def solution(mesh):
    placed = (P("dp", "mp"), P(None, ("mp", "dp")), P("dp"))
    n, n_mp = mesh.shape["dp"], mesh.shape["mp"]
    return jax.shard_map(
        functools.partial(per_device, n, n_mp),
        mesh=mesh,
        in_specs=placed,
        out_specs=P("dp", "mp"),
        check_vma=False,
    )
```

time: 394 us -> 496 us (1.26)
  the two profiles are of different devices: /device:TPU:0 before, /device:TPU:11 now
where the time goes in v3:
time: 496 us; the launch traced here: 494 us
  waiting for transfers between devices  255 us (51%)
  starting transfers between devices  134 us (27%)
  Pallas kernels  57.5 us (12%)
  local copies, waits for them, and re-layouts  21.1 us (4%)
  other arithmetic  20.8 us (4%)
  blocking collectives  5.07 us (1%)
    ppermute x50, waiting for transfers between devices, send(): return lax.ppermute(x, 'dp', [(i, int(plan[step][i])) for i in range(n)])  255 us
    ppermute x50, starting transfers between devices, send(): return lax.ppermute(x, 'dp', [(i, int(plan[step][i])) for i in range(n)])  134 us
    pallas_call x18, Pallas kernels, prune_block(): pl.pallas_call(body, in_specs=in_specs, out_specs=there, scratch_shapes=[...  57.5 us
    dynamic_slice x5, local copies, waits for them, and re-layouts, take(): lax.dynamic_slice(source, (target(step, me, n, jnp.where) * rows + top, 0...  15.3 us
  transfers between devices with their start and end apart: 50, of which 12 were waited for; matrix products, arithmetic and copies ran while one was open for 6% of the time, Pallas kernels for 11%

profile of v3, /device:TPU:11, one launch (start us, length us, event | category | flops | bytes accessed | tf_op | source)
XLA Modules:
  0.0 494.2 jit_solution(12089265795725695465)
XLA Ops:
  1.4 8.5 %multiply_reduce_fusion.1 = f32[14336]{0:T(1024)S(1)} fusion(bf16[512,14336]{1,0:T(8,128)(2,1)} %param.5), kind=kLoop, calls=%fused_computation.3 | loop fusion | flops 22005760 | bytes 14737408 | tf_op jit(solution)/shard_map/reduce_sum | solution.py:114
  22.3 8.6 %collective-permute-start.2 = (f32[896]{0:T(1024)S(1)}, f32[896]{0:T(1024)S(1)}, u32[]{:S(2)}, u32[]{:S(2)}) collective-permute-start(f32[896]{0:T(1024)S(1)} %get-tuple-element.9), channel_id=1, source_target_pairs={{0,10},{2,8},{4,14},{6,12},{8,26},{10,24},{12,30},{14,28},{16,2},{... | collective-permute-start | bytes 10760 | tf_op jit(solution)/shard_map/ppermute | solution.py:100
  31.9 3.4 collective-permute-start.4
  38.1 3.5 collective-permute-start.8
  41.7 9.4 %constant_dynamic-slice_fusion = (bf16[512,896]{1,0:T(8,128)(2,1)}, bf16[512,896]{1,0:T(8,128)(2,1)}, bf16[512,896]{1,0:T(8,128)(2,1)}, bf16[512,896]{1,0:T(8,12...) fusion(bf16[8192,896]{1,0:T(8,128)(2,1)} %param.6, ...), kind=kLoop, calls=%fused_computation.7 | loop fusion | bytes 25690168 | tf_op jit(solution)/shard_map/dynamic_slice | solution.py:103
  56.0 8.2 %multiply_reduce_fusion = f32[8192]{0:T(1024)S(1)} fusion(bf16[8192,896]{1,0:T(8,128)(2,1)S(1)} %bitcast.12, f32[896]{0:T(1024)S(1)} %add_sqrt_fusion), kind=kLoop, calls=%fused_computation.2 | loop fusion | flops 29351936 | bytes 14716416 | tf_op jit(solution)/shard_map/reduce_sum | solution.py:118
  64.9 3.4 collective-permute-start.17
  68.4 26.9 %collective-permute-done.17.note_ref = f32[1,1408]{1,0:T(1,128)S(1)} collective-permute-done((f32[1,1408]{1,0:T(1,128)S(1)}, f32[1,1408]{1,0:T(1,128)S(1)}, u32[]{:S(2)}, u32[]{:S(2)}) %collective-permute-start.17) | collective-permute-done | bytes 5664 | tf_op jit(solution)/shard_map/ppermute | solution.py:100
  120.7 6.9 %collective-permute-start.46 = (bf16[512,896]{1,0:T(8,128)(2,1)}, bf16[512,896]{1,0:T(8,128)(2,1)S(1)}, u32[]{:S(2)}, u32[]{:S(2)}) collective-permute-start(bf16[512,896]{1,0:T(8,128)(2,1)} %get-tuple-element.26), channel_id=1, source_target_pairs={{0,12},{2,14},{4,8},{6,10},{8,28},{10,30},{12,24},{14,26},{16,4},{... | collective-permute-start | bytes 2752520 | tf_op jit(solution)/shard_map/ppermute | solution.py:100
  127.7 4.4 collective-permute-start.45
  132.6 16.0 %collective-permute-done.46.block_ref = bf16[512,896]{1,0:T(8,128)(2,1)S(1)} collective-permute-done((bf16[512,896]{1,0:T(8,128)(2,1)}, bf16[512,896]{1,0:T(8,128)(2,1)S(1)}, u32[]{:S(2)}, u32[]{:S(2)}) %collective-permute-start.46) | collective-permute-done | bytes 917536 | tf_op jit(solution)/shard_map/ppermute | solution.py:100
  148.5 4.4 collective-permute-start.41
  152.9 15.3 %collective-permute-done.45.block_ref = bf16[512,896]{1,0:T(8,128)(2,1)S(1)} collective-permute-done((bf16[512,896]{1,0:T(8,128)(2,1)}, bf16[512,896]{1,0:T(8,128)(2,1)S(1)}, u32[]{:S(2)}, u32[]{:S(2)}) %collective-permute-start.45) | collective-permute-done | bytes 917536 | tf_op jit(solution)/shard_map/ppermute | solution.py:100
  168.3 42.9 %collective-permute-start.40 = (bf16[512,896]{1,0:T(8,128)(2,1)}, bf16[512,896]{1,0:T(8,128)(2,1)}, u32[]{:S(2)}, u32[]{:S(2)}) collective-permute-start(bf16[512,896]{1,0:T(8,128)(2,1)} %get-tuple-element.32), channel_id=1, source_target_pairs={{0,20},{2,22},{4,16},{6,18},{8,4},{10,6},{12,0},{14,2},{16,28},{18... | collective-permute-start | bytes 2752520 | tf_op jit(solution)/shard_map/ppermute | solution.py:100
  211.2 36.7 %collective-permute-done.44.block_ref = bf16[512,896]{1,0:T(8,128)(2,1)} collective-permute-done((bf16[512,896]{1,0:T(8,128)(2,1)}, bf16[512,896]{1,0:T(8,128)(2,1)}, u32[]{:S(2)}, u32[]{:S(2)}) %collective-permute-start.44) | collective-permute-done | bytes 917536 | tf_op jit(solution)/shard_map/ppermute | solution.py:100
  247.9 118.1 %collective-permute-done.43.block_ref = bf16[512,896]{1,0:T(8,128)(2,1)} collective-permute-done((bf16[512,896]{1,0:T(8,128)(2,1)}, bf16[512,896]{1,0:T(8,128)(2,1)}, u32[]{:S(2)}, u32[]{:S(2)}) %collective-permute-start.43) | collective-permute-done | bytes 917536 | tf_op jit(solution)/shard_map/ppermute | solution.py:100
  368.2 8.3 %collective-permute-start.35 = (bf16[512,896]{1,0:T(8,128)(2,1)}, bf16[512,896]{1,0:T(8,128)(2,1)}, u32[]{:S(2)}, u32[]{:S(2)}) collective-permute-start(bf16[512,896]{1,0:T(8,128)(2,1)} %get-tuple-element.37), channel_id=1, source_target_pairs={{0,30},{2,28},{4,26},{6,24},{8,8},{10,10},{12,12},{14,14},{16,16},... | collective-permute-start | bytes 2752520 | tf_op jit(solution)/shard_map/ppermute | solution.py:100
  387.3 35.3 %collective-permute-done.37.block_ref = bf16[512,896]{1,0:T(8,128)(2,1)} collective-permute-done((bf16[512,896]{1,0:T(8,128)(2,1)}, bf16[512,896]{1,0:T(8,128)(2,1)}, u32[]{:S(2)}, u32[]{:S(2)}) %collective-permute-start.37) | collective-permute-done | bytes 917536 | tf_op jit(solution)/shard_map/ppermute | solution.py:100
  422.6 5.0 %collective-permute-start = (bf16[128,896]{1,0:T(8,128)(2,1)S(1)}, bf16[128,896]{1,0:T(8,128)(2,1)S(1)}, u32[]{:S(2)}, u32[]{:S(2)}) collective-permute-start(bf16[128,896]{1,0:T(8,128)(2,1)S(1)} %constant_dynamic-slice_fusion.16), channel_id=1, source_target_pairs={{0,0},{2,2},{4,4},{6,6},{8,22},{10,20},{12,18},{14,16},{16,14},{18... | collective-permute-start | bytes 688136 | tf_op jit(solution)/shard_map/ppermute | solution.py:100
  427.6 5.1 %psum.7 = f32[512]{0:T(512)} all-reduce(f32[512]{0:T(512)} %bitcast.15), channel_id=1, replica_groups=mesh['dp'=16,'mp'=2] {'mp'}, use_global_device_ids=true, to_apply=%region_2.3 | all-reduce | flops 512 | bytes 4096 | tf_op jit(solution)/shard_map/psum | solution.py:121
  441.7 3.4 shard_map.57.rest_0_
  445.1 3.4 shard_map.58.rest_0_
  448.4 3.4 shard_map.59.rest_0_
  451.8 3.4 shard_map.60.rest_0_
  (171 shorter events, 109.5 us)
Async XLA Ops:
  22.3 15.0 %collective-permute-start.2 = (f32[896]{0:T(1024)S(1)}, f32[896]{0:T(1024)S(1)}, u32[]{:S(2)}, u32[]{:S(2)}) collective-permute-start(f32[896]{0:T(1024)S(1)} %get-tuple-element.9), channel_id=1, source_target_pairs={{0,10},{2,8},{4,14},{6,12},{8,26},{10,24},{12,30},{14,28},{16,2},{... | collective-permute-start | bytes 10760 | tf_op jit(solution)/shard_map/ppermute | solution.py:100
  35.3 15.8 %collective-permute-start.5 = (f32[896]{0:T(1024)S(1)}, f32[896]{0:T(1024)S(1)}, u32[]{:S(2)}, u32[]{:S(2)}) collective-permute-start(f32[896]{0:T(1024)S(1)} %get-tuple-element.21), channel_id=1, source_target_pairs={{0,2},{2,0},{4,6},{6,4},{8,16},{10,18},{12,20},{14,22},{16,8},{18,... | collective-permute-start | bytes 10760 | tf_op jit(solution)/shard_map/ppermute | solution.py:100
  35.3 18.2 %collective-permute-start.6 = (f32[896]{0:T(1024)S(1)}, f32[896]{0:T(1024)S(1)}, u32[]{:S(2)}, u32[]{:S(2)}) collective-permute-start(f32[896]{0:T(1024)S(1)} %get-tuple-element.20), channel_id=1, source_target_pairs={{0,4},{2,6},{4,0},{6,2},{8,18},{10,16},{12,22},{14,20},{16,10},{18... | collective-permute-start | bytes 10760 | tf_op jit(solution)/shard_map/ppermute | solution.py:100
  37.3 16.3 %collective-permute-start.7 = (f32[896]{0:T(1024)S(1)}, f32[896]{0:T(1024)S(1)}, u32[]{:S(2)}, u32[]{:S(2)}) collective-permute-start(f32[896]{0:T(1024)S(1)} %get-tuple-element.19), channel_id=1, source_target_pairs={{0,6},{2,4},{4,2},{6,0},{8,20},{10,22},{12,16},{14,18},{16,12},{18... | collective-permute-start | bytes 10760 | tf_op jit(solution)/shard_map/ppermute | solution.py:100
  38.1 17.8 %collective-permute-start.8 = (f32[896]{0:T(1024)S(1)}, f32[896]{0:T(1024)S(1)}, u32[]{:S(2)}, u32[]{:S(2)}) collective-permute-start(f32[896]{0:T(1024)S(1)} %get-tuple-element.18), channel_id=1, source_target_pairs={{0,0},{2,2},{4,4},{6,6},{8,22},{10,20},{12,18},{14,16},{16,14},{18... | collective-permute-start | bytes 10760 | tf_op jit(solution)/shard_map/ppermute | solution.py:100
  51.1 81.0 %collective-permute-start.49 = (bf16[128,896]{1,0:T(8,128)(2,1)S(1)}, bf16[128,896]{1,0:T(8,128)(2,1)S(1)}, u32[]{:S(2)}, u32[]{:S(2)}) collective-permute-start(bf16[128,896]{1,0:T(8,128)(2,1)S(1)} %constant_dynamic-slice_fusion.18), channel_id=1, source_target_pairs={{0,8},{2,10},{4,12},{6,14},{8,24},{10,26},{12,28},{14,30},{16,0},{... | collective-permute-start | bytes 688136 | tf_op jit(solution)/shard_map/ppermute | solution.py:100
  53.5 79.0 %collective-permute-start.48 = (bf16[384,896]{1,0:T(8,128)(2,1)}, bf16[384,896]{1,0:T(8,128)(2,1)}, u32[]{:S(2)}, u32[]{:S(2)}) collective-permute-start(bf16[384,896]{1,0:T(8,128)(2,1)} %constant_dynamic-slice_fusion.17), channel_id=1, source_target_pairs={{0,8},{2,10},{4,12},{6,14},{8,24},{10,26},{12,28},{14,30},{16,0},{... | collective-permute-start | bytes 2064392 | tf_op jit(solution)/shard_map/ppermute | solution.py:100
  53.6 78.9 %collective-permute-start.47 = (bf16[512,896]{1,0:T(8,128)(2,1)}, bf16[512,896]{1,0:T(8,128)(2,1)}, u32[]{:S(2)}, u32[]{:S(2)}) collective-permute-start(bf16[512,896]{1,0:T(8,128)(2,1)} %get-tuple-element.25), channel_id=1, source_target_pairs={{0,10},{2,8},{4,14},{6,12},{8,26},{10,24},{12,30},{14,28},{16,2},{... | collective-permute-start | bytes 2752520 | tf_op jit(solution)/shard_map/ppermute | solution.py:100
  64.9 30.4 %collective-permute-start.17 = (f32[1,1408]{1,0:T(1,128)S(1)}, f32[1,1408]{1,0:T(1,128)S(1)}, u32[]{:S(2)}, u32[]{:S(2)}) collective-permute-start(f32[1,1408]{1,0:T(1,128)S(1)} %get-tuple-element.54), channel_id=1, source_target_pairs={{0,0},{2,2},{4,4},{6,6},{8,22},{10,20},{12,18},{14,16},{16,14},{18... | collective-permute-start | bytes 16904 | tf_op jit(solution)/shard_map/ppermute | solution.py:100
  68.3 26.9 %collective-permute-start.18 = (f32[1,1408]{1,0:T(1,128)S(1)}, f32[1,1408]{1,0:T(1,128)S(1)}, u32[]{:S(2)}, u32[]{:S(2)}) collective-permute-start(f32[1,1408]{1,0:T(1,128)S(1)} %get-tuple-element.39), channel_id=1, source_target_pairs={{0,8},{2,10},{4,12},{6,14},{8,24},{10,26},{12,28},{14,30},{16,0},{... | collective-permute-start | bytes 16904 | tf_op jit(solution)/shard_map/ppermute | solution.py:100
  120.7 27.8 %collective-permute-start.46 = (bf16[512,896]{1,0:T(8,128)(2,1)}, bf16[512,896]{1,0:T(8,128)(2,1)S(1)}, u32[]{:S(2)}, u32[]{:S(2)}) collective-permute-start(bf16[512,896]{1,0:T(8,128)(2,1)} %get-tuple-element.26), channel_id=1, source_target_pairs={{0,12},{2,14},{4,8},{6,10},{8,28},{10,30},{12,24},{14,26},{16,4},{... | collective-permute-start | bytes 2752520 | tf_op jit(solution)/shard_map/ppermute | solution.py:100
  127.7 40.6 %collective-permute-start.45 = (bf16[512,896]{1,0:T(8,128)(2,1)}, bf16[512,896]{1,0:T(8,128)(2,1)S(1)}, u32[]{:S(2)}, u32[]{:S(2)}) collective-permute-start(bf16[512,896]{1,0:T(8,128)(2,1)} %get-tuple-element.27), channel_id=1, source_target_pairs={{0,14},{2,12},{4,10},{6,8},{8,30},{10,28},{12,26},{14,24},{16,6},{... | collective-permute-start | bytes 2752520 | tf_op jit(solution)/shard_map/ppermute | solution.py:100
  132.1 115.8 %collective-permute-start.44 = (bf16[512,896]{1,0:T(8,128)(2,1)}, bf16[512,896]{1,0:T(8,128)(2,1)}, u32[]{:S(2)}, u32[]{:S(2)}) collective-permute-start(bf16[512,896]{1,0:T(8,128)(2,1)} %get-tuple-element.28), channel_id=1, source_target_pairs={{0,2},{2,0},{4,6},{6,4},{8,16},{10,18},{12,20},{14,22},{16,8},{18,... | collective-permute-start | bytes 2752520 | tf_op jit(solution)/shard_map/ppermute | solution.py:100
  132.5 233.6 %collective-permute-start.43 = (bf16[512,896]{1,0:T(8,128)(2,1)}, bf16[512,896]{1,0:T(8,128)(2,1)}, u32[]{:S(2)}, u32[]{:S(2)}) collective-permute-start(bf16[512,896]{1,0:T(8,128)(2,1)} %get-tuple-element.29), channel_id=1, source_target_pairs={{0,4},{2,6},{4,0},{6,2},{8,18},{10,16},{12,22},{14,20},{16,10},{18... | collective-permute-start | bytes 2752520 | tf_op jit(solution)/shard_map/ppermute | solution.py:100
  132.5 233.8 %collective-permute-start.42 = (bf16[512,896]{1,0:T(8,128)(2,1)}, bf16[512,896]{1,0:T(8,128)(2,1)}, u32[]{:S(2)}, u32[]{:S(2)}) collective-permute-start(bf16[512,896]{1,0:T(8,128)(2,1)} %get-tuple-element.30), channel_id=1, source_target_pairs={{0,16},{2,18},{4,20},{6,22},{8,0},{10,2},{12,4},{14,6},{16,24},{18... | collective-permute-start | bytes 2752520 | tf_op jit(solution)/shard_map/ppermute | solution.py:100
  148.5 219.0 %collective-permute-start.41 = (bf16[512,896]{1,0:T(8,128)(2,1)}, bf16[512,896]{1,0:T(8,128)(2,1)}, u32[]{:S(2)}, u32[]{:S(2)}) collective-permute-start(bf16[512,896]{1,0:T(8,128)(2,1)} %get-tuple-element.31), channel_id=1, source_target_pairs={{0,18},{2,16},{4,22},{6,20},{8,2},{10,0},{12,6},{14,4},{16,26},{18... | collective-permute-start | bytes 2752520 | tf_op jit(solution)/shard_map/ppermute | solution.py:100
  168.3 200.0 %collective-permute-start.40 = (bf16[512,896]{1,0:T(8,128)(2,1)}, bf16[512,896]{1,0:T(8,128)(2,1)}, u32[]{:S(2)}, u32[]{:S(2)}) collective-permute-start(bf16[512,896]{1,0:T(8,128)(2,1)} %get-tuple-element.32), channel_id=1, source_target_pairs={{0,20},{2,22},{4,16},{6,18},{8,4},{10,6},{12,0},{14,2},{16,28},{18... | collective-permute-start | bytes 2752520 | tf_op jit(solution)/shard_map/ppermute | solution.py:100
  247.9 128.7 %collective-permute-start.39 = (bf16[512,896]{1,0:T(8,128)(2,1)}, bf16[512,896]{1,0:T(8,128)(2,1)}, u32[]{:S(2)}, u32[]{:S(2)}) collective-permute-start(bf16[512,896]{1,0:T(8,128)(2,1)} %get-tuple-element.33), channel_id=1, source_target_pairs={{0,22},{2,20},{4,18},{6,16},{8,6},{10,4},{12,2},{14,0},{16,30},{18... | collective-permute-start | bytes 2752520 | tf_op jit(solution)/shard_map/ppermute | solution.py:100
  366.3 56.3 %collective-permute-start.37 = (bf16[512,896]{1,0:T(8,128)(2,1)}, bf16[512,896]{1,0:T(8,128)(2,1)}, u32[]{:S(2)}, u32[]{:S(2)}) collective-permute-start(bf16[512,896]{1,0:T(8,128)(2,1)} %get-tuple-element.35), channel_id=1, source_target_pairs={{0,26},{2,24},{4,30},{6,28},{8,12},{10,14},{12,8},{14,10},{16,20},... | collective-permute-start | bytes 2752520 | tf_op jit(solution)/shard_map/ppermute | solution.py:100
  367.5 111.2 %collective-permute-start.36 = (bf16[512,896]{1,0:T(8,128)(2,1)}, bf16[512,896]{1,0:T(8,128)(2,1)}, u32[]{:S(2)}, u32[]{:S(2)}) collective-permute-start(bf16[512,896]{1,0:T(8,128)(2,1)} %get-tuple-element.36), channel_id=1, source_target_pairs={{0,28},{2,30},{4,24},{6,26},{8,14},{10,12},{12,10},{14,8},{16,22},... | collective-permute-start | bytes 2752520 | tf_op jit(solution)/shard_map/ppermute | solution.py:100
  368.2 113.9 %collective-permute-start.35 = (bf16[512,896]{1,0:T(8,128)(2,1)}, bf16[512,896]{1,0:T(8,128)(2,1)}, u32[]{:S(2)}, u32[]{:S(2)}) collective-permute-start(bf16[512,896]{1,0:T(8,128)(2,1)} %get-tuple-element.37), channel_id=1, source_target_pairs={{0,30},{2,28},{4,26},{6,24},{8,8},{10,10},{12,12},{14,14},{16,16},... | collective-permute-start | bytes 2752520 | tf_op jit(solution)/shard_map/ppermute | solution.py:100
  376.6 108.9 %collective-permute-start.34 = (bf16[512,896]{1,0:T(8,128)(2,1)S(1)}, bf16[512,896]{1,0:T(8,128)(2,1)}, u32[]{:S(2)}, u32[]{:S(2)}) collective-permute-start(bf16[512,896]{1,0:T(8,128)(2,1)S(1)} %get-tuple-element.38), channel_id=1, source_target_pairs={{0,6},{2,4},{4,2},{6,0},{8,20},{10,22},{12,16},{14,18},{16,12},{18... | collective-permute-start | bytes 2752520 | tf_op jit(solution)/shard_map/ppermute | solution.py:100
  379.9 108.9 %collective-permute-start.33 = (bf16[384,896]{1,0:T(8,128)(2,1)}, bf16[384,896]{1,0:T(8,128)(2,1)}, u32[]{:S(2)}, u32[]{:S(2)}) collective-permute-start(bf16[384,896]{1,0:T(8,128)(2,1)} %constant_dynamic-slice_fusion.14), channel_id=1, source_target_pairs={{0,0},{2,2},{4,4},{6,6},{8,22},{10,20},{12,18},{14,16},{16,14},{18... | collective-permute-start | bytes 2064392 | tf_op jit(solution)/shard_map/ppermute | solution.py:100
  422.6 68.7 %collective-permute-start = (bf16[128,896]{1,0:T(8,128)(2,1)S(1)}, bf16[128,896]{1,0:T(8,128)(2,1)S(1)}, u32[]{:S(2)}, u32[]{:S(2)}) collective-permute-start(bf16[128,896]{1,0:T(8,128)(2,1)S(1)} %constant_dynamic-slice_fusion.16), channel_id=1, source_target_pairs={{0,0},{2,2},{4,4},{6,6},{8,22},{10,20},{12,18},{14,16},{16,14},{18... | collective-permute-start | bytes 688136 | tf_op jit(solution)/shard_map/ppermute | solution.py:100
  (50 other events, 6365.0 us)

commit v4 on v3

v4 whole, which is shorter than its diff:
```python
import functools

import jax
import jax.numpy as jnp
import numpy as np
from jax import lax
from jax.experimental import pallas as pl
from jax.experimental.pallas import tpu as pltpu
from jax.sharding import PartitionSpec as P


gate_slope = 2.0
small_eps = 1e-06


pairs = (0, 3, 6, 7)


def target(step, i, n, where=np.where):
    if n != 16:
        if n & (n - 1):
            return (i + step) % n
        return i ^ (step + n // 2) % n
    kind = "pair" if step % 8 in pairs else "ring"
    o = sum((k in pairs) == (kind == "pair") for k in range(step % 8))
    place, seat = i >> 2, i & 3
    if kind == "pair":
        inner = (place == 1) | (place == 2)
        return where(inner == (step < 8), 12 - 4 * place + (seat ^ o), i ^ (1, 0, 2, 3)[o])
    hop = ((place & 1) << 1) + ((place >> 1) ^ 1) if step < 8 else (((place & 1) ^ 1) << 1) + (place >> 1)
    return 4 * hop + (seat ^ o)


def source(step, i, n, where=np.where):
    if n != 16:
        return (i - step) % n if n & (n - 1) else target(step, i, n)
    return target(step, i, n, where) if step % 8 in pairs else target((step + 8) % 16, i, n)


def pieces_of(n, rows):
    pieces = []
    for step in range(n):
        if rows % 64 or step != n // 2 - 1:
            pieces.append((step, 0, rows))
        else:
            split = rows - rows // 4
            pieces += [(step, 0, split), (step, split, rows - split)]
    return pieces


near_squares, near_notes = 4, 4


def gather_sums(parts, n, near, extra=None):
    near = near if n % near == 0 else 1
    far = n // near
    inside = [[group * near + member for member in range(near)] for group in range(far)]
    across = [[group * near + member for group in range(far)] for member in range(near)]
    width = parts.shape[1]
    parts = parts.reshape(far, near, width).swapaxes(0, 1)
    if near > 1:
        parts = lax.all_to_all(parts, "dp", 0, 0, axis_index_groups=inside, tiled=True)
    parts = jnp.sum(parts, axis=0)
    if extra is not None:
        parts = jnp.concatenate([parts, jnp.broadcast_to(extra, (far, extra.shape[0]))], axis=1)
    parts = lax.all_to_all(parts, "dp", 0, 0, axis_index_groups=across, tiled=True)
    total = jnp.sum(parts[:, :width], axis=0)
    if extra is None:
        return total
    extras = jnp.broadcast_to(parts[:, width:], (near, far, extra.shape[0]))
    if near > 1:
        extras = lax.all_to_all(extras, "dp", 0, 0, axis_index_groups=inside, tiled=True)
    return total, extras.reshape(n, extra.shape[0])


def prune_block(block, norms, slope, shift, step, top, n, out, near):
    rows, cols = slope.shape[0], block.shape[1]
    size = block.shape[0]
    tile, lines = 128, 128 if near else 32
    parts = size // tile

    def body(block_ref, norms_ref, slope_ref, shift_ref, *rest):
        out_ref, wide_ref, done_ref, in_sem, out_sem = rest[-5:]
        owner = source(step, lax.axis_index("dp"), n, jnp.where)
        at = pl.multiple_of(owner * cols, 128)

        def get(p):
            part = pl.ds(p * tile, tile)
            return pltpu.make_async_copy(block_ref.at[part], wide_ref.at[part], in_sem.at[p])

        def put(p):
            there = out_ref.at[pl.ds(top + p * tile, tile), pl.ds(at, cols)]
            return pltpu.make_async_copy(done_ref.at[pl.ds(p * tile, tile)], there, out_sem.at[p])

        if not near:
            for p in range(parts):
                get(p).start()
        norm = norms_ref[...][step : step + 1, :]
        block_rows = block_ref if near else wide_ref

        @pl.loop(0, parts)
        def _(p):
            if not near:
                get(p).wait()

            @pl.loop(0, tile // lines)
            def _(q):
                first = pl.multiple_of(p * tile + q * lines, lines)
                here, ours = pl.ds(first, lines), pl.ds(top + first, lines)
                wide = block_rows[here].astype(jnp.float32)
                share = jnp.clip(jnp.abs(wide) * norm * slope_ref[ours] + shift_ref[ours], 0.0, 1.0)
                done_ref[here] = (wide * share).astype(jnp.bfloat16)

            put(p).start()

        @pl.loop(0, parts)
        def _(p):
            put(p).wait()

    here, there = pl.BlockSpec(memory_space=pltpu.VMEM), pl.BlockSpec(memory_space=pl.ANY)
    in_specs = [here if near else there, here, here, here]
    if near:
        block = pltpu.with_memory_space_constraint(block, pltpu.VMEM)
    operands = [block, norms, slope, shift]
    if out is not None:
        in_specs.append(there)
        operands.append(out)
    return pl.pallas_call(
        body,
        in_specs=in_specs,
        out_specs=there,
        scratch_shapes=[pltpu.VMEM((size, cols), jnp.bfloat16)] * 2 + [pltpu.SemaphoreType.DMA((parts,))] * 2,
        out_shape=jax.ShapeDtypeStruct((rows, n * cols), jnp.bfloat16),
        input_output_aliases={} if out is None else {4: 0},
        cost_estimate=pl.CostEstimate(flops=6 * size * cols, bytes_accessed=4 * size * cols, transcendentals=0),
    )(*operands)


def per_device(n, n_mp, activations, weight, thresholds):
    ids = np.arange(n)
    plan = [target(k, ids, n) for k in range(n)]
    me = lax.axis_index("dp")
    cols = weight.shape[1]
    rows = weight.shape[0] // n
    total_cols = cols * n * n_mp

    pieces = pieces_of(n, rows)

    def send(x, step):
        return lax.ppermute(x, "dp", [(i, int(plan[step][i])) for i in range(n)])

    def take(rest, step, top, size):
        return lax.dynamic_slice(rest, (target(step, me, n, jnp.where) * rows + top, 0), (size, cols))

    first = take(weight, *pieces[0])
    rest, _ = lax.optimization_barrier((weight, first))
    blocks = [first] + [take(rest, *piece) for piece in pieces[1:]]
    arrived = [send(block, step) for block, (step, _, _) in zip(blocks, pieces)]

    partial_value = jnp.sum(jnp.square(activations.astype(jnp.float32)), axis=0)
    squares = gather_sums(partial_value.reshape(n, cols), n, near_squares)
    col_norm = jnp.sqrt(squares)
    row_part = jnp.sum(jnp.abs(weight.astype(jnp.float32)) * col_norm[None, :], axis=1).reshape(n, rows)
    row_part, norms = gather_sums(row_part, n, near_notes, col_norm)
    by_step = np.stack([source(k, ids, n) for k in range(n)], 1)
    by_step = by_step % near_notes * (n // near_notes) + by_step // near_notes
    by_step = lax.dynamic_index_in_dim(jnp.asarray(by_step.astype(np.int32)), me, 0, keepdims=False)
    norms = jnp.take(norms, by_step, axis=0, mode="clip")
    row_total = lax.psum(row_part, "mp")
    row_mean = row_total / total_cols + small_eps
    slope = (gate_slope / row_mean)[:, None]
    shift = (0.5 - gate_slope * thresholds)[:, None]

    late = [i for i, (step, _, _) in enumerate(pieces) if 5 * n // 16 <= step < n // 2]
    order = [i for i in range(len(pieces)) if i not in late] + late
    if cols % 128 == 0 and rows % 128 == 0:
        norms, slope, shift = [pltpu.with_memory_space_constraint(v, pltpu.VMEM) for v in (norms, slope, shift)]
        out = None
        for i in order:
            step, top, _ = pieces[i]
            near = i in order[-2:]
            out = prune_block(arrived[i], norms, slope, shift, step, top, n, out, near)
        return out
    out = jnp.zeros((rows, n * cols), jnp.bfloat16)
    for i in order:
        step, top, size = pieces[i]
        wide = arrived[i].astype(jnp.float32)
        ours = slice(top, top + size)
        owner = source(step, me, n, jnp.where)
        share = jnp.clip(jnp.abs(wide) * norms[step] * slope[ours] + shift[ours], 0.0, 1.0)
        out = lax.dynamic_update_slice(out, (wide * share).astype(jnp.bfloat16), (top, owner * cols))
    return out


def solution(mesh):
    placed = (P("dp", "mp"), P(None, ("mp", "dp")), P("dp"))
    n, n_mp = mesh.shape["dp"], mesh.shape["mp"]
    return jax.shard_map(
        functools.partial(per_device, n, n_mp),
        mesh=mesh,
        in_specs=placed,
        out_specs=P("dp", "mp"),
        check_vma=False,
    )
```

time: 496 us -> 383 us (0.77)
  the two profiles are of different devices: /device:TPU:11 before, /device:TPU:0 now
where the time goes in v4:
time: 383 us; the launch traced here: 382 us
  waiting for transfers between devices  226 us (59%)
  starting transfers between devices  63.5 us (17%)
  Pallas kernels  49.1 us (13%)
  other arithmetic  19.7 us (5%)
  local copies, waits for them, and re-layouts  18 us (5%)
  blocking collectives  4.91 us (1%)
    all_to_all x2, waiting for transfers between devices, gather_sums(): lax.all_to_all(parts, 'dp', 0, 0, axis_index_groups=across, tiled=True)  152 us
    ppermute x17, waiting for transfers between devices, send(): return lax.ppermute(x, 'dp', [(i, int(plan[step][i])) for i in range(n)])  71.1 us
    pallas_call x17, Pallas kernels, prune_block(): pl.pallas_call(body, in_specs=in_specs, out_specs=there, scratch_shapes=[...  49.1 us
    ppermute x17, starting transfers between devices, send(): return lax.ppermute(x, 'dp', [(i, int(plan[step][i])) for i in range(n)])  33.8 us
    all_to_all x2, starting transfers between devices, gather_sums(): lax.all_to_all(parts, 'dp', 0, 0, axis_index_groups=across, tiled=True)  19.9 us
    dynamic_slice x4, local copies, waits for them, and re-layouts, take(): lax.dynamic_slice(rest, (target(step, me, n, jnp.where) * rows + top, 0),...  13.2 us
    reduce_sum x1, other arithmetic, per_device(): jnp.sum(jnp.abs(weight.astype(jnp.float32)) * col_norm[None, :], axis=1)  11.1 us
    reduce_sum x1, other arithmetic, per_device(): partial_value = jnp.sum(jnp.square(activations.astype(jnp.float32)), axis=0)  8.52 us
  transfers between devices with their start and end apart: 22, of which 7 were waited for; matrix products, arithmetic and copies ran while one was open for 9% of the time, Pallas kernels for 13%

profile of v4, /device:TPU:0, one launch (start us, length us, event | category | flops | bytes accessed | tf_op | source)
XLA Modules:
  0.0 381.8 jit_solution(14654697787844180786)
XLA Ops:
  1.8 9.1 %constant_dynamic-slice_fusion = (bf16[512,896]{1,0:T(8,128)(2,1)S(1)}, bf16[512,896]{1,0:T(8,128)(2,1)}, bf16[512,896]{1,0:T(8,128)(2,1)}, bf16[512,896]{1,0:T(...) fusion(bf16[8192,896]{1,0:T(8,128)(2,1)} %param.5, ...), kind=kLoop, calls=%fused_computation.6 | loop fusion | bytes 25690168 | tf_op jit(solution)/shard_map/dynamic_slice | solution.py:153
  10.9 4.2 %collective-permute-start.15 = (bf16[512,896]{1,0:T(8,128)(2,1)S(1)}, bf16[512,896]{1,0:T(8,128)(2,1)}, u32[]{:S(2)}, u32[]{:S(2)}) collective-permute-start(bf16[512,896]{1,0:T(8,128)(2,1)S(1)} %get-tuple-element.7), channel_id=1, source_target_pairs={{0,8},{2,10},{4,12},{6,14},{8,24},{10,26},{12,28},{14,30},{16,0},{... | collective-permute-start | bytes 2752520 | tf_op jit(solution)/shard_map/ppermute | solution.py:150
  15.9 8.3 %collective-permute-start.13 = (bf16[512,896]{1,0:T(8,128)(2,1)}, bf16[512,896]{1,0:T(8,128)(2,1)}, u32[]{:S(2)}, u32[]{:S(2)}) collective-permute-start(bf16[512,896]{1,0:T(8,128)(2,1)} %get-tuple-element.9), channel_id=1, source_target_pairs={{0,0},{2,2},{4,4},{6,6},{8,18},{10,16},{12,22},{14,20},{16,10},{18... | collective-permute-start | bytes 2752520 | tf_op jit(solution)/shard_map/ppermute | solution.py:150
  24.8 21.9 %collective-permute-done.15.block_ref = bf16[512,896]{1,0:T(8,128)(2,1)} collective-permute-done((bf16[512,896]{1,0:T(8,128)(2,1)S(1)}, bf16[512,896]{1,0:T(8,128)(2,1)}, u32[]{:S(2)}, u32[]{:S(2)}) %collective-permute-start.15) | collective-permute-done | bytes 917536 | tf_op jit(solution)/shard_map/ppermute | solution.py:150
  46.8 8.5 %multiply_reduce_fusion.1 = f32[14336]{0:T(1024)S(1)} fusion(bf16[512,14336]{1,0:T(8,128)(2,1)} %param.4), kind=kLoop, calls=%fused_computation.2 | loop fusion | flops 22005760 | bytes 14737408 | tf_op jit(solution)/shard_map/reduce_sum | solution.py:160
  56.0 3.3 all-to-all-start
  64.0 15.5 %all-to-all-start.1 = ((f32[4,1,896]{2,1,0:T(1,128)}), f32[4,1,896]{2,1,0:T(1,128)S(1)}, u32[]{:S(2)}, u32[]{:S(2)}) async-start(f32[4,1,896]{2,1,0:T(1,128)} %all_to_all.24), calls=%async_computation.1 | async-start | bytes 28672 | tf_op jit(solution)/shard_map/all_to_all | solution.py:66
  81.1 63.1 %all-to-all-done.1 = f32[4,1,896]{2,1,0:T(1,128)S(1)} async-done(((f32[4,1,896]{2,1,0:T(1,128)}), f32[4,1,896]{2,1,0:T(1,128)S(1)}, u32[]{:S(2)}, u32[]{:S(2)}) %all-to-all-start.1) | async-done | bytes 14368 | tf_op jit(solution)/shard_map/all_to_all | solution.py:66
  144.3 4.5 %collective-permute-start.8 = (bf16[512,896]{1,0:T(8,128)(2,1)}, bf16[512,896]{1,0:T(8,128)(2,1)}, u32[]{:S(2)}, u32[]{:S(2)}) collective-permute-start(bf16[512,896]{1,0:T(8,128)(2,1)} %get-tuple-element.14), channel_id=1, source_target_pairs={{0,26},{2,24},{4,30},{6,28},{8,8},{10,10},{12,12},{14,14},{16,16},... | collective-permute-start | bytes 2752520 | tf_op jit(solution)/shard_map/ppermute | solution.py:150
  148.8 6.5 %collective-permute-start.7 = (bf16[512,896]{1,0:T(8,128)(2,1)}, bf16[512,896]{1,0:T(8,128)(2,1)}, u32[]{:S(2)}, u32[]{:S(2)}) collective-permute-start(bf16[512,896]{1,0:T(8,128)(2,1)} %get-tuple-element.15), channel_id=1, source_target_pairs={{0,20},{2,22},{4,16},{6,18},{8,4},{10,6},{12,0},{14,2},{16,28},{18... | collective-permute-start | bytes 2752520 | tf_op jit(solution)/shard_map/ppermute | solution.py:150
  157.7 11.1 %multiply_reduce_fusion = f32[8192]{0:T(1024)S(1)} fusion(bf16[8192,896]{1,0:T(8,128)(2,1)} %param.5, f32[896]{0:T(1024)S(1)} %sqrt.7), kind=kLoop, calls=%fused_computation.1 | loop fusion | flops 29351936 | bytes 14716416 | tf_op jit(solution)/shard_map/reduce_sum | solution.py:163
  169.5 3.3 all-to-all-start.2
  172.7 3.6 collective-permute-start.4
  176.4 11.4 %collective-permute-done.8.block_ref = bf16[512,896]{1,0:T(8,128)(2,1)} collective-permute-done((bf16[512,896]{1,0:T(8,128)(2,1)}, bf16[512,896]{1,0:T(8,128)(2,1)}, u32[]{:S(2)}, u32[]{:S(2)}) %collective-permute-start.8) | collective-permute-done | bytes 917536 | tf_op jit(solution)/shard_map/ppermute | solution.py:150
  187.7 18.5 %collective-permute-done.7.block_ref = bf16[512,896]{1,0:T(8,128)(2,1)} collective-permute-done((bf16[512,896]{1,0:T(8,128)(2,1)}, bf16[512,896]{1,0:T(8,128)(2,1)}, u32[]{:S(2)}, u32[]{:S(2)}) %collective-permute-start.7) | collective-permute-done | bytes 917536 | tf_op jit(solution)/shard_map/ppermute | solution.py:150
  207.4 19.3 %collective-permute-done.6.block_ref = bf16[512,896]{1,0:T(8,128)(2,1)} collective-permute-done((bf16[512,896]{1,0:T(8,128)(2,1)}, bf16[512,896]{1,0:T(8,128)(2,1)}, u32[]{:S(2)}, u32[]{:S(2)}) %collective-permute-start.6) | collective-permute-done | bytes 917536 | tf_op jit(solution)/shard_map/ppermute | solution.py:150
  227.3 4.4 %all-to-all-start.3 = ((f32[4,1,1408]{2,1,0:T(1,128)}), f32[4,1,1408]{2,1,0:T(1,128)S(1)}, u32[]{:S(2)}, u32[]{:S(2)}) async-start(f32[4,1,1408]{2,1,0:T(1,128)} %all_to_all.27), calls=%async_computation.3 | async-start | bytes 45056 | tf_op jit(solution)/shard_map/all_to_all | solution.py:66
  231.9 89.2 %all-to-all-done.3 = f32[4,1,1408]{2,1,0:T(1,128)S(1)} async-done(((f32[4,1,1408]{2,1,0:T(1,128)}), f32[4,1,1408]{2,1,0:T(1,128)S(1)}, u32[]{:S(2)}, u32[]{:S(2)}) %all-to-all-start.3) | async-done | bytes 22560 | tf_op jit(solution)/shard_map/all_to_all | solution.py:66
  321.7 3.3 all-to-all-start.4
  326.8 4.9 %psum.7 = f32[512]{0:T(512)S(1)} all-reduce(f32[512]{0:T(512)S(1)} %slice_reduce_fusion), channel_id=1, replica_groups=mesh['dp'=16,'mp'=2] {'mp'}, use_global_device_ids=true, to_apply=%region_6.7 | all-reduce | flops 512 | bytes 4096 | tf_op jit(solution)/shard_map/psum | solution.py:169
  338.8 3.1 shard_map.48.rest_0_
  341.9 3.1 shard_map.49.rest_0_
  345.1 3.1 shard_map.50.rest_0_
  348.2 3.1 shard_map.51.rest_0_
  (74 shorter events, 55.1 us)
Async XLA Ops:
  1.3 23.0 %collective-permute-start.16 = (bf16[512,896]{1,0:T(8,128)(2,1)S(1)}, bf16[512,896]{1,0:T(8,128)(2,1)S(1)}, u32[]{:S(2)}, u32[]{:S(2)}) collective-permute-start(bf16[512,896]{1,0:T(8,128)(2,1)S(1)} %constant_dynamic-slice_fusion.17), channel_id=1, source_target_pairs={{0,2},{2,0},{4,6},{6,4},{8,16},{10,18},{12,20},{14,22},{16,8},{18,... | collective-permute-start | bytes 2752520 | tf_op jit(solution)/shard_map/ppermute | solution.py:150
  1.8 57.5 %copy-start.2 = (f32[512]{0:T(512)S(1)}, f32[512]{0:T(512)}, u32[]{:S(2)}) copy-start(f32[512]{0:T(512)} %param.6) | copy-start | bytes 6148
  10.9 35.9 %collective-permute-start.15 = (bf16[512,896]{1,0:T(8,128)(2,1)S(1)}, bf16[512,896]{1,0:T(8,128)(2,1)}, u32[]{:S(2)}, u32[]{:S(2)}) collective-permute-start(bf16[512,896]{1,0:T(8,128)(2,1)S(1)} %get-tuple-element.7), channel_id=1, source_target_pairs={{0,8},{2,10},{4,12},{6,14},{8,24},{10,26},{12,28},{14,30},{16,0},{... | collective-permute-start | bytes 2752520 | tf_op jit(solution)/shard_map/ppermute | solution.py:150
  15.1 129.2 %collective-permute-start.14 = (bf16[512,896]{1,0:T(8,128)(2,1)}, bf16[512,896]{1,0:T(8,128)(2,1)}, u32[]{:S(2)}, u32[]{:S(2)}) collective-permute-start(bf16[512,896]{1,0:T(8,128)(2,1)} %get-tuple-element.8), channel_id=1, source_target_pairs={{0,10},{2,8},{4,14},{6,12},{8,26},{10,24},{12,30},{14,28},{16,2},{... | collective-permute-start | bytes 2752520 | tf_op jit(solution)/shard_map/ppermute | solution.py:150
  15.9 128.4 %collective-permute-start.13 = (bf16[512,896]{1,0:T(8,128)(2,1)}, bf16[512,896]{1,0:T(8,128)(2,1)}, u32[]{:S(2)}, u32[]{:S(2)}) collective-permute-start(bf16[512,896]{1,0:T(8,128)(2,1)} %get-tuple-element.9), channel_id=1, source_target_pairs={{0,0},{2,2},{4,4},{6,6},{8,18},{10,16},{12,22},{14,20},{16,10},{18... | collective-permute-start | bytes 2752520 | tf_op jit(solution)/shard_map/ppermute | solution.py:150
  24.3 124.6 %collective-permute-start.12 = (bf16[512,896]{1,0:T(8,128)(2,1)}, bf16[512,896]{1,0:T(8,128)(2,1)}, u32[]{:S(2)}, u32[]{:S(2)}) collective-permute-start(bf16[512,896]{1,0:T(8,128)(2,1)} %get-tuple-element.10), channel_id=1, source_target_pairs={{0,12},{2,14},{4,8},{6,10},{8,28},{10,30},{12,24},{14,26},{16,4},{... | collective-permute-start | bytes 2752520 | tf_op jit(solution)/shard_map/ppermute | solution.py:150
  24.3 144.5 %copy-start = (bf16[512,896]{1,0:T(8,128)(2,1)}, bf16[512,896]{1,0:T(8,128)(2,1)S(1)}, u32[]{:S(2)}) copy-start(bf16[512,896]{1,0:T(8,128)(2,1)S(1)} %collective-permute-done.16.block_ref) | copy-start | bytes 2752516
  24.3 131.1 %collective-permute-start.11 = (bf16[512,896]{1,0:T(8,128)(2,1)}, bf16[512,896]{1,0:T(8,128)(2,1)S(1)}, u32[]{:S(2)}, u32[]{:S(2)}) collective-permute-start(bf16[512,896]{1,0:T(8,128)(2,1)} %get-tuple-element.11), channel_id=1, source_target_pairs={{0,24},{2,26},{4,28},{6,30},{8,10},{10,8},{12,14},{14,12},{16,18},... | collective-permute-start | bytes 2752520 | tf_op jit(solution)/shard_map/ppermute | solution.py:150
  46.8 109.6 %collective-permute-start.10 = (bf16[512,896]{1,0:T(8,128)(2,1)}, bf16[512,896]{1,0:T(8,128)(2,1)}, u32[]{:S(2)}, u32[]{:S(2)}) collective-permute-start(bf16[512,896]{1,0:T(8,128)(2,1)} %get-tuple-element.12), channel_id=1, source_target_pairs={{0,16},{2,18},{4,20},{6,22},{8,0},{10,2},{12,4},{14,6},{16,24},{18... | collective-permute-start | bytes 2752520 | tf_op jit(solution)/shard_map/ppermute | solution.py:150
  56.0 7.3 %all-to-all-start = ((f32[4,4,896]{2,1,0:T(4,128)}), f32[4,4,896]{2,1,0:T(4,128)S(1)}, u32[]{:S(2)}, u32[]{:S(2)}) async-start(f32[4,4,896]{2,1,0:T(4,128)} %copy.89), calls=%async_computation | async-start | bytes 114688 | tf_op jit(solution)/shard_map/all_to_all | solution.py:62
  64.0 80.3 %all-to-all-start.1 = ((f32[4,1,896]{2,1,0:T(1,128)}), f32[4,1,896]{2,1,0:T(1,128)S(1)}, u32[]{:S(2)}, u32[]{:S(2)}) async-start(f32[4,1,896]{2,1,0:T(1,128)} %all_to_all.24), calls=%async_computation.1 | async-start | bytes 28672 | tf_op jit(solution)/shard_map/all_to_all | solution.py:66
  144.3 28.5 %collective-permute-start.9 = (bf16[512,896]{1,0:T(8,128)(2,1)}, bf16[512,896]{1,0:T(8,128)(2,1)}, u32[]{:S(2)}, u32[]{:S(2)}) collective-permute-start(bf16[512,896]{1,0:T(8,128)(2,1)} %get-tuple-element.13), channel_id=1, source_target_pairs={{0,18},{2,16},{4,22},{6,20},{8,2},{10,0},{12,6},{14,4},{16,26},{18... | collective-permute-start | bytes 2752520 | tf_op jit(solution)/shard_map/ppermute | solution.py:150
  144.3 43.4 %collective-permute-start.8 = (bf16[512,896]{1,0:T(8,128)(2,1)}, bf16[512,896]{1,0:T(8,128)(2,1)}, u32[]{:S(2)}, u32[]{:S(2)}) collective-permute-start(bf16[512,896]{1,0:T(8,128)(2,1)} %get-tuple-element.14), channel_id=1, source_target_pairs={{0,26},{2,24},{4,30},{6,28},{8,8},{10,10},{12,12},{14,14},{16,16},... | collective-permute-start | bytes 2752520 | tf_op jit(solution)/shard_map/ppermute | solution.py:150
  148.8 57.3 %collective-permute-start.7 = (bf16[512,896]{1,0:T(8,128)(2,1)}, bf16[512,896]{1,0:T(8,128)(2,1)}, u32[]{:S(2)}, u32[]{:S(2)}) collective-permute-start(bf16[512,896]{1,0:T(8,128)(2,1)} %get-tuple-element.15), channel_id=1, source_target_pairs={{0,20},{2,22},{4,16},{6,18},{8,4},{10,6},{12,0},{14,2},{16,28},{18... | collective-permute-start | bytes 2752520 | tf_op jit(solution)/shard_map/ppermute | solution.py:150
  155.3 71.3 %collective-permute-start.6 = (bf16[512,896]{1,0:T(8,128)(2,1)}, bf16[512,896]{1,0:T(8,128)(2,1)}, u32[]{:S(2)}, u32[]{:S(2)}) collective-permute-start(bf16[512,896]{1,0:T(8,128)(2,1)} %get-tuple-element.16), channel_id=1, source_target_pairs={{0,22},{2,20},{4,18},{6,16},{8,6},{10,4},{12,2},{14,0},{16,30},{18... | collective-permute-start | bytes 2752520 | tf_op jit(solution)/shard_map/ppermute | solution.py:150
  156.4 168.6 %collective-permute-start.5 = (bf16[512,896]{1,0:T(8,128)(2,1)}, bf16[512,896]{1,0:T(8,128)(2,1)}, u32[]{:S(2)}, u32[]{:S(2)}) collective-permute-start(bf16[512,896]{1,0:T(8,128)(2,1)} %get-tuple-element.17), channel_id=1, source_target_pairs={{0,28},{2,30},{4,24},{6,26},{8,12},{10,14},{12,8},{14,10},{16,20},... | collective-permute-start | bytes 2752520 | tf_op jit(solution)/shard_map/ppermute | solution.py:150
  169.5 37.9 %all-to-all-start.2 = ((f32[4,4,512]{2,1,0:T(4,128)}), f32[4,4,512]{2,1,0:T(4,128)S(1)}, u32[]{:S(2)}, u32[]{:S(2)}) async-start(f32[4,4,512]{2,1,0:T(4,128)} %copy.90), calls=%async_computation.2 | async-start | bytes 65536 | tf_op jit(solution)/shard_map/all_to_all | solution.py:62
  172.7 197.4 %collective-permute-start.4 = (bf16[512,896]{1,0:T(8,128)(2,1)}, bf16[512,896]{1,0:T(8,128)(2,1)}, u32[]{:S(2)}, u32[]{:S(2)}) collective-permute-start(bf16[512,896]{1,0:T(8,128)(2,1)} %get-tuple-element.18), channel_id=1, source_target_pairs={{0,30},{2,28},{4,26},{6,24},{8,14},{10,12},{12,10},{14,8},{16,22},... | collective-permute-start | bytes 2752520 | tf_op jit(solution)/shard_map/ppermute | solution.py:150
  187.7 185.6 %collective-permute-start.3 = (bf16[512,896]{1,0:T(8,128)(2,1)}, bf16[512,896]{1,0:T(8,128)(2,1)}, u32[]{:S(2)}, u32[]{:S(2)}) collective-permute-start(bf16[512,896]{1,0:T(8,128)(2,1)} %get-tuple-element.19), channel_id=1, source_target_pairs={{0,14},{2,12},{4,10},{6,8},{8,30},{10,28},{12,26},{14,24},{16,6},{... | collective-permute-start | bytes 2752520 | tf_op jit(solution)/shard_map/ppermute | solution.py:150
  206.2 170.3 %collective-permute-start.2 = (bf16[512,896]{1,0:T(8,128)(2,1)S(1)}, bf16[512,896]{1,0:T(8,128)(2,1)}, u32[]{:S(2)}, u32[]{:S(2)}) collective-permute-start(bf16[512,896]{1,0:T(8,128)(2,1)S(1)} %get-tuple-element.20), channel_id=1, source_target_pairs={{0,4},{2,6},{4,0},{6,2},{8,20},{10,22},{12,16},{14,18},{16,12},{18... | collective-permute-start | bytes 2752520 | tf_op jit(solution)/shard_map/ppermute | solution.py:150
  226.7 152.9 %collective-permute-start.1 = (bf16[384,896]{1,0:T(8,128)(2,1)S(1)}, bf16[384,896]{1,0:T(8,128)(2,1)S(1)}, u32[]{:S(2)}, u32[]{:S(2)}) collective-permute-start(bf16[384,896]{1,0:T(8,128)(2,1)S(1)} %constant_dynamic-slice_fusion.14), channel_id=1, source_target_pairs={{0,6},{2,4},{4,2},{6,0},{8,22},{10,20},{12,18},{14,16},{16,14},{18... | collective-permute-start | bytes 2064392 | tf_op jit(solution)/shard_map/ppermute | solution.py:150
  227.3 93.7 %all-to-all-start.3 = ((f32[4,1,1408]{2,1,0:T(1,128)}), f32[4,1,1408]{2,1,0:T(1,128)S(1)}, u32[]{:S(2)}, u32[]{:S(2)}) async-start(f32[4,1,1408]{2,1,0:T(1,128)} %all_to_all.27), calls=%async_computation.3 | async-start | bytes 45056 | tf_op jit(solution)/shard_map/all_to_all | solution.py:66
  321.7 10.2 %all-to-all-start.4 = ((f32[4,4,896]{2,1,0:T(4,128)}), f32[4,4,896]{2,1,0:T(4,128)S(1)}, u32[]{:S(2)}, u32[]{:S(2)}) async-start(f32[4,4,896]{2,1,0:T(4,128)} %broadcast_in_dim.18), calls=%async_computation.4 | async-start | bytes 114688 | tf_op jit(solution)/shard_map/all_to_all | solution.py:72
  325.1 55.8 %collective-permute-start = (bf16[128,896]{1,0:T(8,128)(2,1)}, bf16[128,896]{1,0:T(8,128)(2,1)S(1)}, u32[]{:S(2)}, u32[]{:S(2)}) collective-permute-start(bf16[128,896]{1,0:T(8,128)(2,1)} %constant_dynamic-slice_fusion.16), channel_id=1, source_target_pairs={{0,6},{2,4},{4,2},{6,0},{8,22},{10,20},{12,18},{14,16},{16,14},{18... | collective-permute-start | bytes 688136 | tf_op jit(solution)/shard_map/ppermute | solution.py:150
  (1 other events, 52.1 us)

commit v5 on v4

--- a/solution.py
+++ b/solution.py
@@ -48,11 +48,12 @@
     return pieces
 
 
-near_squares, near_notes = 4, 4
-
-
-def gather_sums(parts, n, near, extra=None):
-    near = near if n % near == 0 else 1
+def group_size(n):
+    return 4 if n % 4 == 0 else 1
+
+
+def gather_sums(parts, n, extra=None):
+    near = group_size(n)
     far = n // near
     inside = [[group * near + member for member in range(near)] for group in range(far)]
     across = [[group * near + member for group in range(far)] for member in range(near)]
@@ -158,12 +159,12 @@
     arrived = [send(block, step) for block, (step, _, _) in zip(blocks, pieces)]
 
     partial_value = jnp.sum(jnp.square(activations.astype(jnp.float32)), axis=0)
-    squares = gather_sums(partial_value.reshape(n, cols), n, near_squares)
+    squares = gather_sums(partial_value.reshape(n, cols), n)
     col_norm = jnp.sqrt(squares)
     row_part = jnp.sum(jnp.abs(weight.astype(jnp.float32)) * col_norm[None, :], axis=1).reshape(n, rows)
-    row_part, norms = gather_sums(row_part, n, near_notes, col_norm)
+    row_part, norms = gather_sums(row_part, n, col_norm)
     by_step = np.stack([source(k, ids, n) for k in range(n)], 1)
-    by_step = by_step % near_notes * (n // near_notes) + by_step // near_notes
+    by_step = by_step % group_size(n) * (n // group_size(n)) + by_step // group_size(n)
     by_step = lax.dynamic_index_in_dim(jnp.asarray(by_step.astype(np.int32)), me, 0, keepdims=False)
     norms = jnp.take(norms, by_step, axis=0, mode="clip")
     row_total = lax.psum(row_part, "mp")

time: 383 us -> 383 us (level)
  no operation moved by 1% of the time
where the time goes in v5:
time: 383 us; the launch traced here: 382 us
  waiting for transfers between devices  226 us (59%)
  starting transfers between devices  63.5 us (17%)
  Pallas kernels  49.1 us (13%)
  other arithmetic  19.7 us (5%)
  local copies, waits for them, and re-layouts  18 us (5%)
  blocking collectives  4.91 us (1%)
    all_to_all x2, waiting for transfers between devices, gather_sums(): lax.all_to_all(parts, 'dp', 0, 0, axis_index_groups=across, tiled=True)  152 us
    ppermute x17, waiting for transfers between devices, send(): return lax.ppermute(x, 'dp', [(i, int(plan[step][i])) for i in range(n)])  71.1 us
    pallas_call x17, Pallas kernels, prune_block(): pl.pallas_call(body, in_specs=in_specs, out_specs=there, scratch_shapes=[...  49.1 us
    ppermute x17, starting transfers between devices, send(): return lax.ppermute(x, 'dp', [(i, int(plan[step][i])) for i in range(n)])  33.8 us
    all_to_all x2, starting transfers between devices, gather_sums(): lax.all_to_all(parts, 'dp', 0, 0, axis_index_groups=across, tiled=True)  19.9 us
    dynamic_slice x4, local copies, waits for them, and re-layouts, take(): lax.dynamic_slice(rest, (target(step, me, n, jnp.where) * rows + top, 0),...  13.2 us
    reduce_sum x1, other arithmetic, per_device(): jnp.sum(jnp.abs(weight.astype(jnp.float32)) * col_norm[None, :], axis=1)  11.1 us
    reduce_sum x1, other arithmetic, per_device(): partial_value = jnp.sum(jnp.square(activations.astype(jnp.float32)), axis=0)  8.52 us
  transfers between devices with their start and end apart: 22, of which 7 were waited for; matrix products, arithmetic and copies ran while one was open for 9% of the time, Pallas kernels for 13%

profile of v5, /device:TPU:0, one launch (start us, length us, event | category | flops | bytes accessed | tf_op | source)
XLA Modules:
  0.0 381.8 jit_solution(14654697787844180786)
XLA Ops:
  1.8 9.1 %constant_dynamic-slice_fusion = (bf16[512,896]{1,0:T(8,128)(2,1)S(1)}, bf16[512,896]{1,0:T(8,128)(2,1)}, bf16[512,896]{1,0:T(8,128)(2,1)}, bf16[512,896]{1,0:T(...) fusion(bf16[8192,896]{1,0:T(8,128)(2,1)} %param.5, ...), kind=kLoop, calls=%fused_computation.6 | loop fusion | bytes 25690168 | tf_op jit(solution)/shard_map/dynamic_slice | solution.py:154
  10.9 4.2 %collective-permute-start.15 = (bf16[512,896]{1,0:T(8,128)(2,1)S(1)}, bf16[512,896]{1,0:T(8,128)(2,1)}, u32[]{:S(2)}, u32[]{:S(2)}) collective-permute-start(bf16[512,896]{1,0:T(8,128)(2,1)S(1)} %get-tuple-element.7), channel_id=1, source_target_pairs={{0,8},{2,10},{4,12},{6,14},{8,24},{10,26},{12,28},{14,30},{16,0},{... | collective-permute-start | bytes 2752520 | tf_op jit(solution)/shard_map/ppermute | solution.py:151
  15.9 8.3 %collective-permute-start.13 = (bf16[512,896]{1,0:T(8,128)(2,1)}, bf16[512,896]{1,0:T(8,128)(2,1)}, u32[]{:S(2)}, u32[]{:S(2)}) collective-permute-start(bf16[512,896]{1,0:T(8,128)(2,1)} %get-tuple-element.9), channel_id=1, source_target_pairs={{0,0},{2,2},{4,4},{6,6},{8,18},{10,16},{12,22},{14,20},{16,10},{18... | collective-permute-start | bytes 2752520 | tf_op jit(solution)/shard_map/ppermute | solution.py:151
  24.8 21.9 %collective-permute-done.15.block_ref = bf16[512,896]{1,0:T(8,128)(2,1)} collective-permute-done((bf16[512,896]{1,0:T(8,128)(2,1)S(1)}, bf16[512,896]{1,0:T(8,128)(2,1)}, u32[]{:S(2)}, u32[]{:S(2)}) %collective-permute-start.15) | collective-permute-done | bytes 917536 | tf_op jit(solution)/shard_map/ppermute | solution.py:151
  46.8 8.5 %multiply_reduce_fusion.1 = f32[14336]{0:T(1024)S(1)} fusion(bf16[512,14336]{1,0:T(8,128)(2,1)} %param.4), kind=kLoop, calls=%fused_computation.2 | loop fusion | flops 22005760 | bytes 14737408 | tf_op jit(solution)/shard_map/reduce_sum | solution.py:161
  56.0 3.3 all-to-all-start
  64.0 15.5 %all-to-all-start.1 = ((f32[4,1,896]{2,1,0:T(1,128)}), f32[4,1,896]{2,1,0:T(1,128)S(1)}, u32[]{:S(2)}, u32[]{:S(2)}) async-start(f32[4,1,896]{2,1,0:T(1,128)} %all_to_all.24), calls=%async_computation.1 | async-start | bytes 28672 | tf_op jit(solution)/shard_map/all_to_all | solution.py:67
  81.1 63.1 %all-to-all-done.1 = f32[4,1,896]{2,1,0:T(1,128)S(1)} async-done(((f32[4,1,896]{2,1,0:T(1,128)}), f32[4,1,896]{2,1,0:T(1,128)S(1)}, u32[]{:S(2)}, u32[]{:S(2)}) %all-to-all-start.1) | async-done | bytes 14368 | tf_op jit(solution)/shard_map/all_to_all | solution.py:67
  144.3 4.5 %collective-permute-start.8 = (bf16[512,896]{1,0:T(8,128)(2,1)}, bf16[512,896]{1,0:T(8,128)(2,1)}, u32[]{:S(2)}, u32[]{:S(2)}) collective-permute-start(bf16[512,896]{1,0:T(8,128)(2,1)} %get-tuple-element.14), channel_id=1, source_target_pairs={{0,26},{2,24},{4,30},{6,28},{8,8},{10,10},{12,12},{14,14},{16,16},... | collective-permute-start | bytes 2752520 | tf_op jit(solution)/shard_map/ppermute | solution.py:151
  148.8 6.5 %collective-permute-start.7 = (bf16[512,896]{1,0:T(8,128)(2,1)}, bf16[512,896]{1,0:T(8,128)(2,1)}, u32[]{:S(2)}, u32[]{:S(2)}) collective-permute-start(bf16[512,896]{1,0:T(8,128)(2,1)} %get-tuple-element.15), channel_id=1, source_target_pairs={{0,20},{2,22},{4,16},{6,18},{8,4},{10,6},{12,0},{14,2},{16,28},{18... | collective-permute-start | bytes 2752520 | tf_op jit(solution)/shard_map/ppermute | solution.py:151
  157.7 11.1 %multiply_reduce_fusion = f32[8192]{0:T(1024)S(1)} fusion(bf16[8192,896]{1,0:T(8,128)(2,1)} %param.5, f32[896]{0:T(1024)S(1)} %sqrt.7), kind=kLoop, calls=%fused_computation.1 | loop fusion | flops 29351936 | bytes 14716416 | tf_op jit(solution)/shard_map/reduce_sum | solution.py:164
  169.5 3.3 all-to-all-start.2
  172.7 3.6 collective-permute-start.4
  176.4 11.4 %collective-permute-done.8.block_ref = bf16[512,896]{1,0:T(8,128)(2,1)} collective-permute-done((bf16[512,896]{1,0:T(8,128)(2,1)}, bf16[512,896]{1,0:T(8,128)(2,1)}, u32[]{:S(2)}, u32[]{:S(2)}) %collective-permute-start.8) | collective-permute-done | bytes 917536 | tf_op jit(solution)/shard_map/ppermute | solution.py:151
  187.7 18.5 %collective-permute-done.7.block_ref = bf16[512,896]{1,0:T(8,128)(2,1)} collective-permute-done((bf16[512,896]{1,0:T(8,128)(2,1)}, bf16[512,896]{1,0:T(8,128)(2,1)}, u32[]{:S(2)}, u32[]{:S(2)}) %collective-permute-start.7) | collective-permute-done | bytes 917536 | tf_op jit(solution)/shard_map/ppermute | solution.py:151
  207.4 19.3 %collective-permute-done.6.block_ref = bf16[512,896]{1,0:T(8,128)(2,1)} collective-permute-done((bf16[512,896]{1,0:T(8,128)(2,1)}, bf16[512,896]{1,0:T(8,128)(2,1)}, u32[]{:S(2)}, u32[]{:S(2)}) %collective-permute-start.6) | collective-permute-done | bytes 917536 | tf_op jit(solution)/shard_map/ppermute | solution.py:151
  227.3 4.4 %all-to-all-start.3 = ((f32[4,1,1408]{2,1,0:T(1,128)}), f32[4,1,1408]{2,1,0:T(1,128)S(1)}, u32[]{:S(2)}, u32[]{:S(2)}) async-start(f32[4,1,1408]{2,1,0:T(1,128)} %all_to_all.27), calls=%async_computation.3 | async-start | bytes 45056 | tf_op jit(solution)/shard_map/all_to_all | solution.py:67
  231.9 89.2 %all-to-all-done.3 = f32[4,1,1408]{2,1,0:T(1,128)S(1)} async-done(((f32[4,1,1408]{2,1,0:T(1,128)}), f32[4,1,1408]{2,1,0:T(1,128)S(1)}, u32[]{:S(2)}, u32[]{:S(2)}) %all-to-all-start.3) | async-done | bytes 22560 | tf_op jit(solution)/shard_map/all_to_all | solution.py:67
  321.7 3.3 all-to-all-start.4
  326.8 4.9 %psum.7 = f32[512]{0:T(512)S(1)} all-reduce(f32[512]{0:T(512)S(1)} %slice_reduce_fusion), channel_id=1, replica_groups=mesh['dp'=16,'mp'=2] {'mp'}, use_global_device_ids=true, to_apply=%region_6.7 | all-reduce | flops 512 | bytes 4096 | tf_op jit(solution)/shard_map/psum | solution.py:170
  338.8 3.1 shard_map.48.rest_0_
  341.9 3.1 shard_map.49.rest_0_
  345.1 3.1 shard_map.50.rest_0_
  348.2 3.1 shard_map.51.rest_0_
  (74 shorter events, 55.1 us)
Async XLA Ops:
  1.3 23.0 %collective-permute-start.16 = (bf16[512,896]{1,0:T(8,128)(2,1)S(1)}, bf16[512,896]{1,0:T(8,128)(2,1)S(1)}, u32[]{:S(2)}, u32[]{:S(2)}) collective-permute-start(bf16[512,896]{1,0:T(8,128)(2,1)S(1)} %constant_dynamic-slice_fusion.17), channel_id=1, source_target_pairs={{0,2},{2,0},{4,6},{6,4},{8,16},{10,18},{12,20},{14,22},{16,8},{18,... | collective-permute-start | bytes 2752520 | tf_op jit(solution)/shard_map/ppermute | solution.py:151
  1.8 57.5 %copy-start.2 = (f32[512]{0:T(512)S(1)}, f32[512]{0:T(512)}, u32[]{:S(2)}) copy-start(f32[512]{0:T(512)} %param.6) | copy-start | bytes 6148
  10.9 35.9 %collective-permute-start.15 = (bf16[512,896]{1,0:T(8,128)(2,1)S(1)}, bf16[512,896]{1,0:T(8,128)(2,1)}, u32[]{:S(2)}, u32[]{:S(2)}) collective-permute-start(bf16[512,896]{1,0:T(8,128)(2,1)S(1)} %get-tuple-element.7), channel_id=1, source_target_pairs={{0,8},{2,10},{4,12},{6,14},{8,24},{10,26},{12,28},{14,30},{16,0},{... | collective-permute-start | bytes 2752520 | tf_op jit(solution)/shard_map/ppermute | solution.py:151
  15.1 129.2 %collective-permute-start.14 = (bf16[512,896]{1,0:T(8,128)(2,1)}, bf16[512,896]{1,0:T(8,128)(2,1)}, u32[]{:S(2)}, u32[]{:S(2)}) collective-permute-start(bf16[512,896]{1,0:T(8,128)(2,1)} %get-tuple-element.8), channel_id=1, source_target_pairs={{0,10},{2,8},{4,14},{6,12},{8,26},{10,24},{12,30},{14,28},{16,2},{... | collective-permute-start | bytes 2752520 | tf_op jit(solution)/shard_map/ppermute | solution.py:151
  15.9 128.4 %collective-permute-start.13 = (bf16[512,896]{1,0:T(8,128)(2,1)}, bf16[512,896]{1,0:T(8,128)(2,1)}, u32[]{:S(2)}, u32[]{:S(2)}) collective-permute-start(bf16[512,896]{1,0:T(8,128)(2,1)} %get-tuple-element.9), channel_id=1, source_target_pairs={{0,0},{2,2},{4,4},{6,6},{8,18},{10,16},{12,22},{14,20},{16,10},{18... | collective-permute-start | bytes 2752520 | tf_op jit(solution)/shard_map/ppermute | solution.py:151
  24.3 124.6 %collective-permute-start.12 = (bf16[512,896]{1,0:T(8,128)(2,1)}, bf16[512,896]{1,0:T(8,128)(2,1)}, u32[]{:S(2)}, u32[]{:S(2)}) collective-permute-start(bf16[512,896]{1,0:T(8,128)(2,1)} %get-tuple-element.10), channel_id=1, source_target_pairs={{0,12},{2,14},{4,8},{6,10},{8,28},{10,30},{12,24},{14,26},{16,4},{... | collective-permute-start | bytes 2752520 | tf_op jit(solution)/shard_map/ppermute | solution.py:151
  24.3 144.5 %copy-start = (bf16[512,896]{1,0:T(8,128)(2,1)}, bf16[512,896]{1,0:T(8,128)(2,1)S(1)}, u32[]{:S(2)}) copy-start(bf16[512,896]{1,0:T(8,128)(2,1)S(1)} %collective-permute-done.16.block_ref) | copy-start | bytes 2752516
  24.3 131.1 %collective-permute-start.11 = (bf16[512,896]{1,0:T(8,128)(2,1)}, bf16[512,896]{1,0:T(8,128)(2,1)S(1)}, u32[]{:S(2)}, u32[]{:S(2)}) collective-permute-start(bf16[512,896]{1,0:T(8,128)(2,1)} %get-tuple-element.11), channel_id=1, source_target_pairs={{0,24},{2,26},{4,28},{6,30},{8,10},{10,8},{12,14},{14,12},{16,18},... | collective-permute-start | bytes 2752520 | tf_op jit(solution)/shard_map/ppermute | solution.py:151
  46.8 109.6 %collective-permute-start.10 = (bf16[512,896]{1,0:T(8,128)(2,1)}, bf16[512,896]{1,0:T(8,128)(2,1)}, u32[]{:S(2)}, u32[]{:S(2)}) collective-permute-start(bf16[512,896]{1,0:T(8,128)(2,1)} %get-tuple-element.12), channel_id=1, source_target_pairs={{0,16},{2,18},{4,20},{6,22},{8,0},{10,2},{12,4},{14,6},{16,24},{18... | collective-permute-start | bytes 2752520 | tf_op jit(solution)/shard_map/ppermute | solution.py:151
  56.0 7.3 %all-to-all-start = ((f32[4,4,896]{2,1,0:T(4,128)}), f32[4,4,896]{2,1,0:T(4,128)S(1)}, u32[]{:S(2)}, u32[]{:S(2)}) async-start(f32[4,4,896]{2,1,0:T(4,128)} %copy.89), calls=%async_computation | async-start | bytes 114688 | tf_op jit(solution)/shard_map/all_to_all | solution.py:63
  64.0 80.3 %all-to-all-start.1 = ((f32[4,1,896]{2,1,0:T(1,128)}), f32[4,1,896]{2,1,0:T(1,128)S(1)}, u32[]{:S(2)}, u32[]{:S(2)}) async-start(f32[4,1,896]{2,1,0:T(1,128)} %all_to_all.24), calls=%async_computation.1 | async-start | bytes 28672 | tf_op jit(solution)/shard_map/all_to_all | solution.py:67
  144.3 28.5 %collective-permute-start.9 = (bf16[512,896]{1,0:T(8,128)(2,1)}, bf16[512,896]{1,0:T(8,128)(2,1)}, u32[]{:S(2)}, u32[]{:S(2)}) collective-permute-start(bf16[512,896]{1,0:T(8,128)(2,1)} %get-tuple-element.13), channel_id=1, source_target_pairs={{0,18},{2,16},{4,22},{6,20},{8,2},{10,0},{12,6},{14,4},{16,26},{18... | collective-permute-start | bytes 2752520 | tf_op jit(solution)/shard_map/ppermute | solution.py:151
  144.3 43.4 %collective-permute-start.8 = (bf16[512,896]{1,0:T(8,128)(2,1)}, bf16[512,896]{1,0:T(8,128)(2,1)}, u32[]{:S(2)}, u32[]{:S(2)}) collective-permute-start(bf16[512,896]{1,0:T(8,128)(2,1)} %get-tuple-element.14), channel_id=1, source_target_pairs={{0,26},{2,24},{4,30},{6,28},{8,8},{10,10},{12,12},{14,14},{16,16},... | collective-permute-start | bytes 2752520 | tf_op jit(solution)/shard_map/ppermute | solution.py:151
  148.8 57.3 %collective-permute-start.7 = (bf16[512,896]{1,0:T(8,128)(2,1)}, bf16[512,896]{1,0:T(8,128)(2,1)}, u32[]{:S(2)}, u32[]{:S(2)}) collective-permute-start(bf16[512,896]{1,0:T(8,128)(2,1)} %get-tuple-element.15), channel_id=1, source_target_pairs={{0,20},{2,22},{4,16},{6,18},{8,4},{10,6},{12,0},{14,2},{16,28},{18... | collective-permute-start | bytes 2752520 | tf_op jit(solution)/shard_map/ppermute | solution.py:151
  155.3 71.3 %collective-permute-start.6 = (bf16[512,896]{1,0:T(8,128)(2,1)}, bf16[512,896]{1,0:T(8,128)(2,1)}, u32[]{:S(2)}, u32[]{:S(2)}) collective-permute-start(bf16[512,896]{1,0:T(8,128)(2,1)} %get-tuple-element.16), channel_id=1, source_target_pairs={{0,22},{2,20},{4,18},{6,16},{8,6},{10,4},{12,2},{14,0},{16,30},{18... | collective-permute-start | bytes 2752520 | tf_op jit(solution)/shard_map/ppermute | solution.py:151
  156.4 168.6 %collective-permute-start.5 = (bf16[512,896]{1,0:T(8,128)(2,1)}, bf16[512,896]{1,0:T(8,128)(2,1)}, u32[]{:S(2)}, u32[]{:S(2)}) collective-permute-start(bf16[512,896]{1,0:T(8,128)(2,1)} %get-tuple-element.17), channel_id=1, source_target_pairs={{0,28},{2,30},{4,24},{6,26},{8,12},{10,14},{12,8},{14,10},{16,20},... | collective-permute-start | bytes 2752520 | tf_op jit(solution)/shard_map/ppermute | solution.py:151
  169.5 37.9 %all-to-all-start.2 = ((f32[4,4,512]{2,1,0:T(4,128)}), f32[4,4,512]{2,1,0:T(4,128)S(1)}, u32[]{:S(2)}, u32[]{:S(2)}) async-start(f32[4,4,512]{2,1,0:T(4,128)} %copy.90), calls=%async_computation.2 | async-start | bytes 65536 | tf_op jit(solution)/shard_map/all_to_all | solution.py:63
  172.7 197.4 %collective-permute-start.4 = (bf16[512,896]{1,0:T(8,128)(2,1)}, bf16[512,896]{1,0:T(8,128)(2,1)}, u32[]{:S(2)}, u32[]{:S(2)}) collective-permute-start(bf16[512,896]{1,0:T(8,128)(2,1)} %get-tuple-element.18), channel_id=1, source_target_pairs={{0,30},{2,28},{4,26},{6,24},{8,14},{10,12},{12,10},{14,8},{16,22},... | collective-permute-start | bytes 2752520 | tf_op jit(solution)/shard_map/ppermute | solution.py:151
  187.7 185.6 %collective-permute-start.3 = (bf16[512,896]{1,0:T(8,128)(2,1)}, bf16[512,896]{1,0:T(8,128)(2,1)}, u32[]{:S(2)}, u32[]{:S(2)}) collective-permute-start(bf16[512,896]{1,0:T(8,128)(2,1)} %get-tuple-element.19), channel_id=1, source_target_pairs={{0,14},{2,12},{4,10},{6,8},{8,30},{10,28},{12,26},{14,24},{16,6},{... | collective-permute-start | bytes 2752520 | tf_op jit(solution)/shard_map/ppermute | solution.py:151
  206.2 170.3 %collective-permute-start.2 = (bf16[512,896]{1,0:T(8,128)(2,1)S(1)}, bf16[512,896]{1,0:T(8,128)(2,1)}, u32[]{:S(2)}, u32[]{:S(2)}) collective-permute-start(bf16[512,896]{1,0:T(8,128)(2,1)S(1)} %get-tuple-element.20), channel_id=1, source_target_pairs={{0,4},{2,6},{4,0},{6,2},{8,20},{10,22},{12,16},{14,18},{16,12},{18... | collective-permute-start | bytes 2752520 | tf_op jit(solution)/shard_map/ppermute | solution.py:151
  226.7 152.9 %collective-permute-start.1 = (bf16[384,896]{1,0:T(8,128)(2,1)S(1)}, bf16[384,896]{1,0:T(8,128)(2,1)S(1)}, u32[]{:S(2)}, u32[]{:S(2)}) collective-permute-start(bf16[384,896]{1,0:T(8,128)(2,1)S(1)} %constant_dynamic-slice_fusion.14), channel_id=1, source_target_pairs={{0,6},{2,4},{4,2},{6,0},{8,22},{10,20},{12,18},{14,16},{16,14},{18... | collective-permute-start | bytes 2064392 | tf_op jit(solution)/shard_map/ppermute | solution.py:151
  227.3 93.7 %all-to-all-start.3 = ((f32[4,1,1408]{2,1,0:T(1,128)}), f32[4,1,1408]{2,1,0:T(1,128)S(1)}, u32[]{:S(2)}, u32[]{:S(2)}) async-start(f32[4,1,1408]{2,1,0:T(1,128)} %all_to_all.27), calls=%async_computation.3 | async-start | bytes 45056 | tf_op jit(solution)/shard_map/all_to_all | solution.py:67
  321.7 10.2 %all-to-all-start.4 = ((f32[4,4,896]{2,1,0:T(4,128)}), f32[4,4,896]{2,1,0:T(4,128)S(1)}, u32[]{:S(2)}, u32[]{:S(2)}) async-start(f32[4,4,896]{2,1,0:T(4,128)} %broadcast_in_dim.18), calls=%async_computation.4 | async-start | bytes 114688 | tf_op jit(solution)/shard_map/all_to_all | solution.py:73
  325.1 55.8 %collective-permute-start = (bf16[128,896]{1,0:T(8,128)(2,1)}, bf16[128,896]{1,0:T(8,128)(2,1)S(1)}, u32[]{:S(2)}, u32[]{:S(2)}) collective-permute-start(bf16[128,896]{1,0:T(8,128)(2,1)} %constant_dynamic-slice_fusion.16), channel_id=1, source_target_pairs={{0,6},{2,4},{4,2},{6,0},{8,22},{10,20},{12,18},{14,16},{16,14},{18... | collective-permute-start | bytes 688136 | tf_op jit(solution)/shard_map/ppermute | solution.py:151
  (1 other events, 52.1 us)

commit v6 on v5

--- a/solution.py
+++ b/solution.py
@@ -40,10 +40,10 @@
 def pieces_of(n, rows):
     pieces = []
     for step in range(n):
-        if rows % 64 or step != n // 2 - 1:
+        if rows % 64 or step not in (0, n // 2 - 1):
             pieces.append((step, 0, rows))
         else:
-            split = rows - rows // 4
+            split = rows - rows // 4 if step else rows // 4
             pieces += [(step, 0, split), (step, split, rows - split)]
     return pieces
 
@@ -74,6 +74,22 @@
     return total, extras.reshape(n, extra.shape[0])
 
 
+def take_ahead(weight, step, top, size, n, rows):
+    def body(weight_ref, out_ref, sem):
+        start = pl.multiple_of(target(step, lax.axis_index("dp"), n, jnp.where) * rows + top, 128)
+        copy = pltpu.make_async_copy(weight_ref.at[pl.ds(start, size)], out_ref, sem)
+        copy.start()
+        copy.wait()
+
+    return pl.pallas_call(
+        body,
+        in_specs=[pl.BlockSpec(memory_space=pl.ANY)],
+        out_specs=pl.BlockSpec(memory_space=pltpu.VMEM),
+        scratch_shapes=[pltpu.SemaphoreType.DMA],
+        out_shape=pltpu.VMEM((size, weight.shape[1]), weight.dtype),
+    )(weight)
+
+
 def prune_block(block, norms, slope, shift, step, top, n, out, near):
     rows, cols = slope.shape[0], block.shape[1]
     size = block.shape[0]
@@ -153,9 +169,12 @@
     def take(rest, step, top, size):
         return lax.dynamic_slice(rest, (target(step, me, n, jnp.where) * rows + top, 0), (size, cols))
 
-    first = take(weight, *pieces[0])
-    rest, _ = lax.optimization_barrier((weight, first))
-    blocks = [first] + [take(rest, *piece) for piece in pieces[1:]]
+    blocks, rest = [], weight
+    for i, piece in enumerate(pieces):
+        ahead = i < 2 and cols % 128 == 0 and rows % 512 == 0
+        blocks.append(take_ahead(rest, *piece, n, rows) if ahead else take(rest, *piece))
+        if i < 2:
+            rest, _ = lax.optimization_barrier((rest, blocks[-1]))
     arrived = [send(block, step) for block, (step, _, _) in zip(blocks, pieces)]
 
     partial_value = jnp.sum(jnp.square(activations.astype(jnp.float32)), axis=0)

time: 383 us -> 395 us (1.031)
  starting transfers between devices: 63.5 us -> 90.2 us
  waiting for transfers between devices: 226 us -> 208 us
    ppermute x17 -> x18, starting transfers between devices: 33.8 us -> 72.3 us  [send(): return lax.ppermute(x, 'dp', [(i, int(plan[step][i])) for i in range(n)])]
    ppermute x17 -> x18, waiting for transfers between devices: 71.1 us -> 47.8 us  [send(): return lax.ppermute(x, 'dp', [(i, int(plan[step][i])) for i in range(n)])]
    all_to_all x2, starting transfers between devices: 19.9 us -> 8.06 us  [gather_sums(): lax.all_to_all(parts, 'dp', 0, 0, axis_index_groups=across, tiled=True)]
    all_to_all x2, waiting for transfers between devices: 152 us -> 158 us  [gather_sums(): lax.all_to_all(parts, 'dp', 0, 0, axis_index_groups=across, tiled=True)]
    pallas_call x17 -> x18, Pallas kernels: 49.1 us -> 50.7 us  [prune_block(): pl.pallas_call(body, in_specs=in_specs, out_specs=there, scratch_shapes=[...]
    dynamic_slice x4 -> x3, local copies, waits for them, and re-layouts: 13.2 us -> 12.5 us  [take(): lax.dynamic_slice(rest, (target(step, me, n, jnp.where) * rows + top, 0),...]
  transfers between devices with their start and end apart: 22 -> 23, of which waited for: 7 -> 6; matrix products, arithmetic and copies ran while one was open for 9% -> 7% of each run, Pallas kernels for 13% -> 13%
where the time goes in v6:
time: 395 us; the launch traced here: 393 us
  waiting for transfers between devices  208 us (53%)
  starting transfers between devices  90.2 us (23%)
  Pallas kernels  52.8 us (13%)
  other arithmetic  19.7 us (5%)
  local copies, waits for them, and re-layouts  17.3 us (4%)
  blocking collectives  4.91 us (1%)
    all_to_all x2, waiting for transfers between devices, gather_sums(): lax.all_to_all(parts, 'dp', 0, 0, axis_index_groups=across, tiled=True)  158 us
    ppermute x18, starting transfers between devices, send(): return lax.ppermute(x, 'dp', [(i, int(plan[step][i])) for i in range(n)])  72.3 us
    pallas_call x18, Pallas kernels, prune_block(): pl.pallas_call(body, in_specs=in_specs, out_specs=there, scratch_shapes=[...  50.7 us
    ppermute x18, waiting for transfers between devices, send(): return lax.ppermute(x, 'dp', [(i, int(plan[step][i])) for i in range(n)])  47.8 us
    dynamic_slice x3, local copies, waits for them, and re-layouts, take(): lax.dynamic_slice(rest, (target(step, me, n, jnp.where) * rows + top, 0),...  12.5 us
    reduce_sum x1, other arithmetic, per_device(): jnp.sum(jnp.abs(weight.astype(jnp.float32)) * col_norm[None, :], axis=1)  11.1 us
    reduce_sum x1, other arithmetic, per_device(): partial_value = jnp.sum(jnp.square(activations.astype(jnp.float32)), axis=0)  8.52 us
    all_to_all x2, starting transfers between devices, gather_sums(): lax.all_to_all(parts, 'dp', 0, 0, axis_index_groups=across, tiled=True)  8.06 us
  transfers between devices with their start and end apart: 23, of which 6 were waited for; matrix products, arithmetic and copies ran while one was open for 7% of the time, Pallas kernels for 13%

profile of v6, /device:TPU:0, one launch (start us, length us, event | category | flops | bytes accessed | tf_op | source)
XLA Modules:
  0.0 393.3 jit_solution(9518386928904852068)
XLA Ops:
  2.2 8.8 %constant_dynamic-slice_fusion = (bf16[512,896]{1,0:T(8,128)(2,1)S(1)}, bf16[512,896]{1,0:T(8,128)(2,1)}, bf16[512,896]{1,0:T(8,128)(2,1)}, bf16[512,896]{1,0:T(...) fusion(bf16[8192,896]{1,0:T(8,128)(2,1)} %weight_ref.2, ...), kind=kLoop, calls=%fused_computation.6 | loop fusion | bytes 25690168 | tf_op jit(solution)/shard_map/dynamic_slice | solution.py:170
  17.3 8.3 %collective-permute-start.13 = (bf16[512,896]{1,0:T(8,128)(2,1)}, bf16[512,896]{1,0:T(8,128)(2,1)}, u32[]{:S(2)}, u32[]{:S(2)}) collective-permute-start(bf16[512,896]{1,0:T(8,128)(2,1)} %get-tuple-element.11), channel_id=1, source_target_pairs={{0,0},{2,2},{4,4},{6,6},{8,18},{10,16},{12,22},{14,20},{16,10},{18... | collective-permute-start | bytes 2752520 | tf_op jit(solution)/shard_map/ppermute | solution.py:167
  25.7 32.4 %collective-permute-start.12 = (bf16[512,896]{1,0:T(8,128)(2,1)}, bf16[512,896]{1,0:T(8,128)(2,1)}, u32[]{:S(2)}, u32[]{:S(2)}) collective-permute-start(bf16[512,896]{1,0:T(8,128)(2,1)} %get-tuple-element.12), channel_id=1, source_target_pairs={{0,12},{2,14},{4,8},{6,10},{8,28},{10,30},{12,24},{14,26},{16,4},{... | collective-permute-start | bytes 2752520 | tf_op jit(solution)/shard_map/ppermute | solution.py:167
  58.1 3.4 collective-permute-start.11
  61.5 8.5 %multiply_reduce_fusion.1 = f32[14336]{0:T(1024)S(1)} fusion(bf16[512,14336]{1,0:T(8,128)(2,1)} %param.4), kind=kLoop, calls=%fused_computation.2 | loop fusion | flops 22005760 | bytes 14737408 | tf_op jit(solution)/shard_map/reduce_sum | solution.py:180
  70.7 3.3 all-to-all-start
  78.7 3.6 all-to-all-start.1
  84.0 69.9 %all-to-all-done.1 = f32[4,1,896]{2,1,0:T(1,128)S(1)} async-done(((f32[4,1,896]{2,1,0:T(1,128)}), f32[4,1,896]{2,1,0:T(1,128)S(1)}, u32[]{:S(2)}, u32[]{:S(2)}) %all-to-all-start.1) | async-done | bytes 14368 | tf_op jit(solution)/shard_map/all_to_all | solution.py:67
  154.9 3.9 collective-permute-start.8
  158.8 7.3 %collective-permute-start.7 = (bf16[512,896]{1,0:T(8,128)(2,1)}, bf16[512,896]{1,0:T(8,128)(2,1)}, u32[]{:S(2)}, u32[]{:S(2)}) collective-permute-start(bf16[512,896]{1,0:T(8,128)(2,1)} %get-tuple-element.17), channel_id=1, source_target_pairs={{0,20},{2,22},{4,16},{6,18},{8,4},{10,6},{12,0},{14,2},{16,28},{18... | collective-permute-start | bytes 2752520 | tf_op jit(solution)/shard_map/ppermute | solution.py:167
  167.3 11.1 %multiply_reduce_fusion = f32[8192]{0:T(1024)S(1)} fusion(bf16[8192,896]{1,0:T(8,128)(2,1)} %weight_ref.2, f32[896]{0:T(1024)S(1)} %sqrt.7), kind=kLoop, calls=%fused_computation.1 | loop fusion | flops 29351936 | bytes 14716416 | tf_op jit(solution)/shard_map/reduce_sum | solution.py:183
  179.0 3.3 all-to-all-start.2
  182.3 4.8 %collective-permute-start.4 = (bf16[512,896]{1,0:T(8,128)(2,1)}, bf16[512,896]{1,0:T(8,128)(2,1)}, u32[]{:S(2)}, u32[]{:S(2)}) collective-permute-start(bf16[512,896]{1,0:T(8,128)(2,1)} %get-tuple-element.20), channel_id=1, source_target_pairs={{0,30},{2,28},{4,26},{6,24},{8,14},{10,12},{12,10},{14,8},{16,22},... | collective-permute-start | bytes 2752520 | tf_op jit(solution)/shard_map/ppermute | solution.py:167
  187.1 9.7 %collective-permute-done.8.block_ref = bf16[512,896]{1,0:T(8,128)(2,1)} collective-permute-done((bf16[512,896]{1,0:T(8,128)(2,1)}, bf16[512,896]{1,0:T(8,128)(2,1)}, u32[]{:S(2)}, u32[]{:S(2)}) %collective-permute-start.8) | collective-permute-done | bytes 917536 | tf_op jit(solution)/shard_map/ppermute | solution.py:167
  196.8 19.2 %collective-permute-done.7.block_ref = bf16[512,896]{1,0:T(8,128)(2,1)} collective-permute-done((bf16[512,896]{1,0:T(8,128)(2,1)}, bf16[512,896]{1,0:T(8,128)(2,1)}, u32[]{:S(2)}, u32[]{:S(2)}) %collective-permute-start.7) | collective-permute-done | bytes 917536 | tf_op jit(solution)/shard_map/ppermute | solution.py:167
  217.6 18.9 %collective-permute-done.6.block_ref = bf16[512,896]{1,0:T(8,128)(2,1)} collective-permute-done((bf16[512,896]{1,0:T(8,128)(2,1)}, bf16[512,896]{1,0:T(8,128)(2,1)}, u32[]{:S(2)}, u32[]{:S(2)}) %collective-permute-start.6) | collective-permute-done | bytes 917536 | tf_op jit(solution)/shard_map/ppermute | solution.py:167
  238.1 4.4 %all-to-all-start.3 = ((f32[4,1,1408]{2,1,0:T(1,128)}), f32[4,1,1408]{2,1,0:T(1,128)S(1)}, u32[]{:S(2)}, u32[]{:S(2)}) async-start(f32[4,1,1408]{2,1,0:T(1,128)} %all_to_all.27), calls=%async_computation.3 | async-start | bytes 45056 | tf_op jit(solution)/shard_map/all_to_all | solution.py:67
  242.7 88.3 %all-to-all-done.3 = f32[4,1,1408]{2,1,0:T(1,128)S(1)} async-done(((f32[4,1,1408]{2,1,0:T(1,128)}), f32[4,1,1408]{2,1,0:T(1,128)S(1)}, u32[]{:S(2)}, u32[]{:S(2)}) %all-to-all-start.3) | async-done | bytes 22560 | tf_op jit(solution)/shard_map/all_to_all | solution.py:67
  331.7 3.3 all-to-all-start.4
  336.8 4.9 %psum.7 = f32[512]{0:T(512)S(1)} all-reduce(f32[512]{0:T(512)S(1)} %slice_reduce_fusion), channel_id=1, replica_groups=mesh['dp'=16,'mp'=2] {'mp'}, use_global_device_ids=true, to_apply=%region_6.7 | all-reduce | flops 512 | bytes 4096 | tf_op jit(solution)/shard_map/psum | solution.py:189
  347.2 3.1 shard_map.50.rest_0_
  350.4 3.1 shard_map.51.rest_0_
  353.5 3.1 shard_map.52.rest_0_
  356.6 3.1 shard_map.53.rest_0_
  (80 shorter events, 63.1 us)
Async XLA Ops:
  2.2 71.9 %copy-start.3 = (f32[512]{0:T(512)S(1)}, f32[512]{0:T(512)}, u32[]{:S(2)}) copy-start(f32[512]{0:T(512)} %param.6) | copy-start | bytes 6148
  11.0 50.4 %collective-permute-start.15 = (bf16[512,896]{1,0:T(8,128)(2,1)S(1)}, bf16[512,896]{1,0:T(8,128)(2,1)}, u32[]{:S(2)}, u32[]{:S(2)}) collective-permute-start(bf16[512,896]{1,0:T(8,128)(2,1)S(1)} %get-tuple-element.9), channel_id=1, source_target_pairs={{0,8},{2,10},{4,12},{6,14},{8,24},{10,26},{12,28},{14,30},{16,0},{... | collective-permute-start | bytes 2752520 | tf_op jit(solution)/shard_map/ppermute | solution.py:167
  14.1 44.0 %collective-permute-start.16 = (bf16[384,896]{1,0:T(8,128)(2,1)S(1)}, bf16[384,896]{1,0:T(8,128)(2,1)S(1)}, u32[]{:S(2)}, u32[]{:S(2)}) collective-permute-start(bf16[384,896]{1,0:T(8,128)(2,1)S(1)} %shard_map.47), channel_id=1, source_target_pairs={{0,2},{2,0},{4,6},{6,4},{8,16},{10,18},{12,20},{14,22},{16,8},{18,... | collective-permute-start | bytes 2064392 | tf_op jit(solution)/shard_map/ppermute | solution.py:167
  14.1 11.5 %collective-permute-start.17 = (bf16[128,896]{1,0:T(8,128)(2,1)S(1)}, bf16[128,896]{1,0:T(8,128)(2,1)S(1)}, u32[]{:S(2)}, u32[]{:S(2)}) collective-permute-start(bf16[128,896]{1,0:T(8,128)(2,1)S(1)} %shard_map.46), channel_id=1, source_target_pairs={{0,2},{2,0},{4,6},{6,4},{8,16},{10,18},{12,20},{14,22},{16,8},{18,... | collective-permute-start | bytes 688136 | tf_op jit(solution)/shard_map/ppermute | solution.py:167
  14.6 139.2 %collective-permute-start.14 = (bf16[512,896]{1,0:T(8,128)(2,1)}, bf16[512,896]{1,0:T(8,128)(2,1)}, u32[]{:S(2)}, u32[]{:S(2)}) collective-permute-start(bf16[512,896]{1,0:T(8,128)(2,1)} %get-tuple-element.10), channel_id=1, source_target_pairs={{0,10},{2,8},{4,14},{6,12},{8,26},{10,24},{12,30},{14,28},{16,2},{... | collective-permute-start | bytes 2752520 | tf_op jit(solution)/shard_map/ppermute | solution.py:167
  17.3 137.5 %collective-permute-start.13 = (bf16[512,896]{1,0:T(8,128)(2,1)}, bf16[512,896]{1,0:T(8,128)(2,1)}, u32[]{:S(2)}, u32[]{:S(2)}) collective-permute-start(bf16[512,896]{1,0:T(8,128)(2,1)} %get-tuple-element.11), channel_id=1, source_target_pairs={{0,0},{2,2},{4,4},{6,6},{8,18},{10,16},{12,22},{14,20},{16,10},{18... | collective-permute-start | bytes 2752520 | tf_op jit(solution)/shard_map/ppermute | solution.py:167
  25.7 133.1 %collective-permute-start.12 = (bf16[512,896]{1,0:T(8,128)(2,1)}, bf16[512,896]{1,0:T(8,128)(2,1)}, u32[]{:S(2)}, u32[]{:S(2)}) collective-permute-start(bf16[512,896]{1,0:T(8,128)(2,1)} %get-tuple-element.12), channel_id=1, source_target_pairs={{0,12},{2,14},{4,8},{6,10},{8,28},{10,30},{12,24},{14,26},{16,4},{... | collective-permute-start | bytes 2752520 | tf_op jit(solution)/shard_map/ppermute | solution.py:167
  58.1 108.0 %collective-permute-start.11 = (bf16[512,896]{1,0:T(8,128)(2,1)}, bf16[512,896]{1,0:T(8,128)(2,1)S(1)}, u32[]{:S(2)}, u32[]{:S(2)}) collective-permute-start(bf16[512,896]{1,0:T(8,128)(2,1)} %get-tuple-element.13), channel_id=1, source_target_pairs={{0,24},{2,26},{4,28},{6,30},{8,10},{10,8},{12,14},{14,12},{16,18},... | collective-permute-start | bytes 2752520 | tf_op jit(solution)/shard_map/ppermute | solution.py:167
  61.5 105.7 %collective-permute-start.10 = (bf16[512,896]{1,0:T(8,128)(2,1)}, bf16[512,896]{1,0:T(8,128)(2,1)}, u32[]{:S(2)}, u32[]{:S(2)}) collective-permute-start(bf16[512,896]{1,0:T(8,128)(2,1)} %get-tuple-element.14), channel_id=1, source_target_pairs={{0,16},{2,18},{4,20},{6,22},{8,0},{10,2},{12,4},{14,6},{16,24},{18... | collective-permute-start | bytes 2752520 | tf_op jit(solution)/shard_map/ppermute | solution.py:167
  70.7 7.3 %all-to-all-start = ((f32[4,4,896]{2,1,0:T(4,128)}), f32[4,4,896]{2,1,0:T(4,128)S(1)}, u32[]{:S(2)}, u32[]{:S(2)}) async-start(f32[4,4,896]{2,1,0:T(4,128)} %copy.94), calls=%async_computation | async-start | bytes 114688 | tf_op jit(solution)/shard_map/all_to_all | solution.py:63
  78.7 75.1 %all-to-all-start.1 = ((f32[4,1,896]{2,1,0:T(1,128)}), f32[4,1,896]{2,1,0:T(1,128)S(1)}, u32[]{:S(2)}, u32[]{:S(2)}) async-start(f32[4,1,896]{2,1,0:T(1,128)} %all_to_all.24), calls=%async_computation.1 | async-start | bytes 28672 | tf_op jit(solution)/shard_map/all_to_all | solution.py:67
  153.9 28.5 %collective-permute-start.9 = (bf16[512,896]{1,0:T(8,128)(2,1)}, bf16[512,896]{1,0:T(8,128)(2,1)}, u32[]{:S(2)}, u32[]{:S(2)}) collective-permute-start(bf16[512,896]{1,0:T(8,128)(2,1)} %get-tuple-element.15), channel_id=1, source_target_pairs={{0,18},{2,16},{4,22},{6,20},{8,2},{10,0},{12,6},{14,4},{16,26},{18... | collective-permute-start | bytes 2752520 | tf_op jit(solution)/shard_map/ppermute | solution.py:167
  154.9 42.0 %collective-permute-start.8 = (bf16[512,896]{1,0:T(8,128)(2,1)}, bf16[512,896]{1,0:T(8,128)(2,1)}, u32[]{:S(2)}, u32[]{:S(2)}) collective-permute-start(bf16[512,896]{1,0:T(8,128)(2,1)} %get-tuple-element.16), channel_id=1, source_target_pairs={{0,26},{2,24},{4,30},{6,28},{8,8},{10,10},{12,12},{14,14},{16,16},... | collective-permute-start | bytes 2752520 | tf_op jit(solution)/shard_map/ppermute | solution.py:167
  158.8 57.3 %collective-permute-start.7 = (bf16[512,896]{1,0:T(8,128)(2,1)}, bf16[512,896]{1,0:T(8,128)(2,1)}, u32[]{:S(2)}, u32[]{:S(2)}) collective-permute-start(bf16[512,896]{1,0:T(8,128)(2,1)} %get-tuple-element.17), channel_id=1, source_target_pairs={{0,20},{2,22},{4,16},{6,18},{8,4},{10,6},{12,0},{14,2},{16,28},{18... | collective-permute-start | bytes 2752520 | tf_op jit(solution)/shard_map/ppermute | solution.py:167
  166.1 70.3 %collective-permute-start.6 = (bf16[512,896]{1,0:T(8,128)(2,1)}, bf16[512,896]{1,0:T(8,128)(2,1)}, u32[]{:S(2)}, u32[]{:S(2)}) collective-permute-start(bf16[512,896]{1,0:T(8,128)(2,1)} %get-tuple-element.18), channel_id=1, source_target_pairs={{0,22},{2,20},{4,18},{6,16},{8,6},{10,4},{12,2},{14,0},{16,30},{18... | collective-permute-start | bytes 2752520 | tf_op jit(solution)/shard_map/ppermute | solution.py:167
  167.2 167.8 %collective-permute-start.5 = (bf16[512,896]{1,0:T(8,128)(2,1)}, bf16[512,896]{1,0:T(8,128)(2,1)}, u32[]{:S(2)}, u32[]{:S(2)}) collective-permute-start(bf16[512,896]{1,0:T(8,128)(2,1)} %get-tuple-element.19), channel_id=1, source_target_pairs={{0,28},{2,30},{4,24},{6,26},{8,12},{10,14},{12,8},{14,10},{16,20},... | collective-permute-start | bytes 2752520 | tf_op jit(solution)/shard_map/ppermute | solution.py:167
  179.0 38.5 %all-to-all-start.2 = ((f32[4,4,512]{2,1,0:T(4,128)}), f32[4,4,512]{2,1,0:T(4,128)S(1)}, u32[]{:S(2)}, u32[]{:S(2)}) async-start(f32[4,4,512]{2,1,0:T(4,128)} %copy.95), calls=%async_computation.2 | async-start | bytes 65536 | tf_op jit(solution)/shard_map/all_to_all | solution.py:63
  182.3 199.4 %collective-permute-start.4 = (bf16[512,896]{1,0:T(8,128)(2,1)}, bf16[512,896]{1,0:T(8,128)(2,1)}, u32[]{:S(2)}, u32[]{:S(2)}) collective-permute-start(bf16[512,896]{1,0:T(8,128)(2,1)} %get-tuple-element.20), channel_id=1, source_target_pairs={{0,30},{2,28},{4,26},{6,24},{8,14},{10,12},{12,10},{14,8},{16,22},... | collective-permute-start | bytes 2752520 | tf_op jit(solution)/shard_map/ppermute | solution.py:167
  196.8 188.1 %collective-permute-start.3 = (bf16[512,896]{1,0:T(8,128)(2,1)S(1)}, bf16[512,896]{1,0:T(8,128)(2,1)}, u32[]{:S(2)}, u32[]{:S(2)}) collective-permute-start(bf16[512,896]{1,0:T(8,128)(2,1)S(1)} %get-tuple-element.21), channel_id=1, source_target_pairs={{0,14},{2,12},{4,10},{6,8},{8,30},{10,28},{12,26},{14,24},{16,6},{... | collective-permute-start | bytes 2752520 | tf_op jit(solution)/shard_map/ppermute | solution.py:167
  216.0 172.0 %collective-permute-start.2 = (bf16[512,896]{1,0:T(8,128)(2,1)S(1)}, bf16[512,896]{1,0:T(8,128)(2,1)}, u32[]{:S(2)}, u32[]{:S(2)}) collective-permute-start(bf16[512,896]{1,0:T(8,128)(2,1)S(1)} %get-tuple-element.22), channel_id=1, source_target_pairs={{0,4},{2,6},{4,0},{6,2},{8,20},{10,22},{12,16},{14,18},{16,12},{18... | collective-permute-start | bytes 2752520 | tf_op jit(solution)/shard_map/ppermute | solution.py:167
  236.4 154.8 %collective-permute-start.1 = (bf16[384,896]{1,0:T(8,128)(2,1)}, bf16[384,896]{1,0:T(8,128)(2,1)S(1)}, u32[]{:S(2)}, u32[]{:S(2)}) collective-permute-start(bf16[384,896]{1,0:T(8,128)(2,1)} %constant_dynamic-slice_fusion.14), channel_id=1, source_target_pairs={{0,6},{2,4},{4,2},{6,0},{8,22},{10,20},{12,18},{14,16},{16,14},{18... | collective-permute-start | bytes 2064392 | tf_op jit(solution)/shard_map/ppermute | solution.py:167
  238.1 92.9 %all-to-all-start.3 = ((f32[4,1,1408]{2,1,0:T(1,128)}), f32[4,1,1408]{2,1,0:T(1,128)S(1)}, u32[]{:S(2)}, u32[]{:S(2)}) async-start(f32[4,1,1408]{2,1,0:T(1,128)} %all_to_all.27), calls=%async_computation.3 | async-start | bytes 45056 | tf_op jit(solution)/shard_map/all_to_all | solution.py:67
  331.7 10.2 %all-to-all-start.4 = ((f32[4,4,896]{2,1,0:T(4,128)}), f32[4,4,896]{2,1,0:T(4,128)S(1)}, u32[]{:S(2)}, u32[]{:S(2)}) async-start(f32[4,4,896]{2,1,0:T(4,128)} %broadcast_in_dim.18), calls=%async_computation.4 | async-start | bytes 114688 | tf_op jit(solution)/shard_map/all_to_all | solution.py:73
  335.0 57.5 %collective-permute-start = (bf16[128,896]{1,0:T(8,128)(2,1)}, bf16[128,896]{1,0:T(8,128)(2,1)S(1)}, u32[]{:S(2)}, u32[]{:S(2)}) collective-permute-start(bf16[128,896]{1,0:T(8,128)(2,1)} %constant_dynamic-slice_fusion.16), channel_id=1, source_target_pairs={{0,6},{2,4},{4,2},{6,0},{8,22},{10,20},{12,18},{14,16},{16,14},{18... | collective-permute-start | bytes 688136 | tf_op jit(solution)/shard_map/ppermute | solution.py:167
  (3 other events, 90.7 us)
